TPU v7x, 128 devices: a whole 4x4x4 slice. The times are simulated.
128 devices in a mesh: gx: 8 (over x, core), gy: 16 (over z, y).
Axes of the slice: x: 4, y: 4, z: 4, core: 2. Of those that a mesh axis runs over, the one named last changes fastest.
Arguments:
- state_init: float32 [4, 32, 64, 2048], P(None, None, 'gx', 'gy'), may hold values from -6 to 6
- right_side: float32 [4, 32, 64, 2048], P(None, None, 'gx', 'gy'), may hold values from -6 to 6
- rock_type: int32 [32, 64, 2048], P(None, 'gx', 'gy'), may hold values from 0 to 7
- trans_table: float32 [4, 8], replicated, may hold values from 0.25 to 4
- perf_cells: int32 [128, 128, 128], P(('gx', 'gy')), may hold values from 0 to 32767
- seg_slot: int32 [4096, 256], P(('gx', 'gy')), may hold values from 0 to 16383, as said below
- seg_inverse: float32 [4, 4, 4096, 256], P(None, None, ('gx', 'gy')), may hold values from -3 to 3
Outputs:
- state_final: float32 [4, 32, 64, 2048], P(None, None, 'gx', 'gy')
- well_rates: float32 [4, 4096, 256], P(None, ('gx', 'gy'))
Inputs may be any that keep to these rules, and one draw needn't show every extreme that they name: `seg_slot`: for each owner (the wells w with the same w // 32) the positions of its segments are distinct; from each source device they name the first slots, at most 128 of them, and for every owner some source fills all 128.
All inputs are finite; a program needn't handle non-finite values.
Results may differ from a plain program's by a relative error of at most 0.0003.
Values sent between devices are 32-bit elements; how exact they have to be, the bound alone decides.
A program may use at most 128 MiB of HBM per device.

v0:
```python
import jax
import jax.numpy as jnp
from jax import lax
from jax.sharding import PartitionSpec as P

NEWTON = 2
SWEEPS = 4


def extended(block, sides, width):
    for axis, dim in sides:
        count = lax.axis_size(axis)
        forward = [(i, i + 1) for i in range(count - 1)]
        backward = [(target, source) for source, target in forward]
        low = lax.ppermute(
            lax.slice_in_dim(block, block.shape[dim] - width, None, axis=dim), axis, forward
        )
        high = lax.ppermute(lax.slice_in_dim(block, 0, width, axis=dim), axis, backward)
        block = jnp.concatenate([low, block, high], axis=dim)
    return block


def coefficient(rock_type, trans_table):
    total = jnp.zeros((trans_table.shape[0],) + rock_type.shape, jnp.float32)
    for rock_kind in range(trans_table.shape[1]):
        picked = jnp.where(rock_type == rock_kind, 1.0, 0.0).astype(jnp.float32)
        total = total + picked[None] * trans_table[:, rock_kind][:, None, None, None]
    return 6.0 + total


def decay_matrix(count):
    first = jnp.arange(count, dtype=jnp.int32)[:, None]
    second = jnp.arange(count, dtype=jnp.int32)[None, :]
    gap = (second - first).astype(jnp.float32)
    return jnp.where(gap >= 0, 0.3 * jnp.power(jnp.float32(0.9), jnp.maximum(gap, 0.0)), 0.0)


def neighbour_sum(padded):
    total = padded[:, 2:, 1:-1, 1:-1] + padded[:, :-2, 1:-1, 1:-1]
    total = total + padded[:, 1:-1, 2:, 1:-1] + padded[:, 1:-1, :-2, 1:-1]
    return total + padded[:, 1:-1, 1:-1, 2:] + padded[:, 1:-1, 1:-1, :-2]


def vertical_pad(lateral):
    return jnp.pad(lateral, ((0, 0), (1, 1), (0, 0), (0, 0)))


def segment_rates(rows, seg_inverse, decay):
    flow = jnp.sum(seg_inverse * rows[None], axis=1)
    shaped = flow.reshape(-1, flow.shape[2])
    return jnp.dot(shaped, decay, precision=lax.Precision.HIGHEST).reshape(flow.shape)


def to_owners(buffer):
    return lax.all_to_all(buffer, ("gx", "gy"), split_axis=1, concat_axis=1, tiled=True)


def to_cells(buffer):
    return lax.all_to_all(buffer, ("gx", "gy"), split_axis=1, concat_axis=1, tiled=True)


def smooth(forcing, jacobi):
    correction = forcing / jacobi
    for sweep_step in range(SWEEPS - 1):
        rimmed = extended(correction, (("gx", 2), ("gy", 3)), 1)
        correction = (forcing + neighbour_sum(vertical_pad(rimmed))) / jacobi
    return correction


def on_device(state_init, right_side, rock_type, trans_table, perf_cells, seg_slot, seg_inverse):
    channels = state_init.shape[0]
    devices = perf_cells.shape[1]
    capacity = perf_cells.shape[2]
    well_count = seg_slot.shape[0]
    seg_count = seg_slot.shape[1]
    coeff = coefficient(rock_type, trans_table)
    decay = decay_matrix(seg_count)
    cell_index = perf_cells.reshape(-1)
    positions = seg_slot.reshape(-1)
    state = state_init
    rates = jnp.zeros((channels, well_count, seg_count), jnp.float32)
    for newton_step in range(NEWTON):
        flat_state = state.reshape(channels, -1)
        outgoing = flat_state[:, cell_index].reshape(channels, devices, capacity)
        incoming = to_owners(outgoing).reshape(channels, -1)
        seg_rows = incoming[:, positions].reshape(channels, well_count, seg_count)
        rates = segment_rates(seg_rows, seg_inverse, decay)
        returned = (
            jnp.zeros((channels, devices * capacity), jnp.float32)
            .at[:, positions]
            .set(rates.reshape(channels, -1))
        )
        arrived = to_cells(returned.reshape(channels, devices, capacity)).reshape(channels, -1)
        inflow = jnp.zeros_like(flat_state).at[:, cell_index].add(arrived).reshape(state.shape)
        lateral = extended(state, (("gx", 2), ("gy", 3)), 1)
        forcing = (
            coeff * state
            - neighbour_sum(vertical_pad(lateral))
            + 0.1 * state * state * state
            - right_side
            - inflow
        )
        jacobi = coeff + 0.3 * state * state
        correction = smooth(forcing, jacobi)
        state = state - correction
    return (state, rates)


def solution(mesh):
    in_specs = (
        P(None, None, "gx", "gy"),
        P(None, None, "gx", "gy"),
        P(None, "gx", "gy"),
        P(),
        P(("gx", "gy"), None, None),
        P(("gx", "gy"), None),
        P(None, None, ("gx", "gy"), None),
    )
    out_specs = (P(None, None, "gx", "gy"), P(None, ("gx", "gy"), None))
    return jax.shard_map(
        on_device, mesh=mesh, in_specs=in_specs, out_specs=out_specs, check_vma=False
    )
```

profile of v0, /device:TPU:1, one launch (start us, length us, event | category | flops | bytes accessed | tf_op | source)
XLA Modules:
  0.0 772.6 jit_solution(15929558001809059731)
XLA Ops:
  1.6 9.6 %copy.207 = f32[4,32,8,128]{0,3,2,1:T(8,128)} copy(f32[4,32,8,128]{3,2,1,0:T(8,128)} %param.7) | data formatting | bytes 1048576 | tf_op args[0]
  11.2 60.6 %gather_fusion = f32[16384,4]{1,0:T(8,128)} fusion(f32[4,32768]{0,1:T(8,128)} %bitcast.48, s32[16384]{0:T(1024)S(1)} %broadcast_clamp_fusion), kind=kCustom, calls=%fused_computation | custom fusion | bytes 589824 | tf_op jit(solution)/shard_map/gather | solution.py:84
  71.8 6.0 copy.208
  77.8 11.5 %all-to-all-start = ((f32[4,128,128]{2,0,1:T(4,128)}), f32[4,128,128]{2,0,1:T(4,128)S(1)}, u32[]{:S(2)}, u32[]{:S(2)}) async-start(f32[4,128,128]{2,0,1:T(4,128)} %copy.208), calls=%async_computation | async-start | bytes 524288 | tf_op jit(solution)/shard_map/all_to_all | solution.py:55
  111.6 31.3 %gather_fusion.1 = f32[8192,4]{1,0:T(8,128)} fusion(f32[4,16384]{0,1:T(8,128)} %bitcast.51, s32[8192]{0:T(1024)S(1)} %broadcast_clamp_fusion.1), kind=kCustom, calls=%fused_computation.1 | custom fusion | bytes 294912 | tf_op jit(solution)/shard_map/gather | solution.py:86
  149.0 24.9 %scatter_custom_fusion = f32[4,16384]{0,1:T(8,128)} fusion(s32[8192]{0:T(1024)S(1)} %bitcast.63, f32[4,8192]{0,1:T(8,128)} %copy.211, f32[]{:T(128)} %constant.18.clone.1), kind=kCustom, calls=%fused_computation.15 | custom fusion | bytes 393220 | tf_op jit(solution)/shard_map/scatter | solution.py:91
  173.9 5.9 copy.212
  179.8 11.2 %all-to-all-start.1 = ((f32[4,128,128]{2,0,1:T(4,128)}), f32[4,128,128]{2,0,1:T(4,128)S(1)}, u32[]{:S(2)}, u32[]{:S(2)}) async-start(f32[4,128,128]{2,0,1:T(4,128)} %copy.212), calls=%async_computation.1 | async-start | bytes 524288 | tf_op jit(solution)/shard_map/all_to_all | solution.py:59
  207.6 94.4 %scatter_custom_fusion.1 = f32[4,32768]{0,1:T(8,128)} fusion(s32[16384]{0:T(1024)} %bitcast.59, f32[16384,4]{1,0:T(8,128)} %copy.213, f32[]{:T(128)} %constant.18.clone.1), kind=kCustom, calls=%fused_computation.10 | custom fusion | flops 65536 | bytes 524800 | tf_op jit(solution)/shard_map/scatter-add | solution.py:94
  302.1 10.8 %copy.214 = f32[4,32,8,128]{3,1,2,0:T(8,128)} copy(f32[4,32,8,128]{0,3,2,1:T(8,128)} %bitcast.45) | data formatting | bytes 1048576 | tf_op jit(solution)/shard_map/reshape | solution.py:94
  343.1 5.6 collective-permute-start.8
  368.2 5.7 collective-permute-start.12
  393.1 8.7 %copy.243 = f32[4,32,8,128]{0,3,2,1:T(8,128)} copy(f32[4,32,8,128]{3,1,2,0:T(8,128)S(1)} %fusion.46) | data formatting | bytes 1048576 | tf_op jit(solution)/shard_map/sub | solution.py:105
  401.8 60.6 %gather_fusion.2 = f32[16384,4]{1,0:T(8,128)} fusion(f32[4,32768]{0,1:T(8,128)} %bitcast.49, s32[16384]{0:T(1024)S(1)} %copy-done.23), kind=kCustom, calls=%fused_computation.2 | custom fusion | bytes 589824 | tf_op jit(solution)/shard_map/gather | solution.py:84
  462.4 5.9 copy.244
  468.3 13.2 %all-to-all-start.2 = ((f32[4,128,128]{2,0,1:T(4,128)}), f32[4,128,128]{2,0,1:T(4,128)S(1)}, u32[]{:S(2)}, u32[]{:S(2)}) async-start(f32[4,128,128]{2,0,1:T(4,128)} %copy.244), calls=%async_computation.2 | async-start | bytes 524288 | tf_op jit(solution)/shard_map/all_to_all | solution.py:55
  497.8 31.2 %gather_fusion.3 = f32[8192,4]{1,0:T(8,128)} fusion(f32[4,16384]{0,1:T(8,128)} %bitcast.50, s32[8192]{0:T(1024)S(1)} %copy-done.31), kind=kCustom, calls=%fused_computation.3 | custom fusion | bytes 294912 | tf_op jit(solution)/shard_map/gather | solution.py:86
  535.2 24.9 %scatter_custom_fusion.2 = f32[4,16384]{0,1:T(8,128)} fusion(s32[8192]{0:T(1024)} %bitcast.64, f32[4,8192]{0,1:T(8,128)} %copy.247, f32[]{:T(128)} %constant.18.clone.1), kind=kCustom, calls=%fused_computation.13 | custom fusion | bytes 4456960 | tf_op jit(solution)/shard_map/scatter | solution.py:91
  560.1 5.9 copy.248
  566.0 7.4 all-to-all-start.3
  591.1 94.4 %scatter_custom_fusion.3 = f32[4,32768]{0,1:T(8,128)} fusion(s32[16384]{0:T(1024)} %bitcast.60, f32[16384,4]{1,0:T(8,128)} %copy.249, f32[]{:T(128)} %constant.18.clone.1), kind=kCustom, calls=%fused_computation.8 | custom fusion | flops 65536 | bytes 524800 | tf_op jit(solution)/shard_map/scatter-add | solution.py:94
  685.5 10.8 %copy.250 = f32[4,32,8,128]{3,1,2,0:T(8,128)} copy(f32[4,32,8,128]{0,3,2,1:T(8,128)} %bitcast.44) | data formatting | bytes 1048576 | tf_op jit(solution)/shard_map/reshape | solution.py:94
  724.0 5.2 collective-permute-start.24
  748.9 5.4 collective-permute-start.28
  (249 shorter events, 219.7 us)
Async XLA Ops:
  77.8 29.0 %all-to-all-start = ((f32[4,128,128]{2,0,1:T(4,128)}), f32[4,128,128]{2,0,1:T(4,128)S(1)}, u32[]{:S(2)}, u32[]{:S(2)}) async-start(f32[4,128,128]{2,0,1:T(4,128)} %copy.208), calls=%async_computation | async-start | bytes 524288 | tf_op jit(solution)/shard_map/all_to_all | solution.py:55
  89.4 7.8 %collective-permute-start.1 = (f32[4,32,1,128]{3,1,2,0:T(8,128)S(1)}, f32[4,32,1,128]{3,1,2,0:T(8,128)S(1)}, u32[]{:S(2)}, u32[]{:S(2)}) collective-permute-start(f32[4,32,1,128]{3,1,2,0:T(8,128)S(1)} %get-tuple-element.54), channel_id=1, source_target_pairs={{16,0},{32,16},{48,32},{64,48},{80,64},{96,80},{112,96},{17,1},{33... | collective-permute-start | bytes 196616 | tf_op jit(solution)/shard_map/ppermute | solution.py:18
  102.2 97.8 %collective-permute-start.2 = (f32[4,32,10,1]{1,2,3,0:T(8,128)S(1)}, f32[4,32,10,1]{1,2,3,0:T(8,128)S(1)}, u32[]{:S(2)}, u32[]{:S(2)}) collective-permute-start(f32[4,32,10,1]{1,2,3,0:T(8,128)S(1)} %get-tuple-element.24), channel_id=1, source_target_pairs={{0,1},{1,2},{2,3},{3,4},{4,5},{5,6},{6,7},{7,8},{8,9},{9,10},{10,1... | collective-permute-start | bytes 15368 | tf_op jit(solution)/shard_map/ppermute | solution.py:15
  105.5 94.9 %collective-permute-start.3 = (f32[4,32,10,1]{1,2,3,0:T(8,128)S(1)}, f32[4,32,10,1]{1,2,3,0:T(8,128)S(1)}, u32[]{:S(2)}, u32[]{:S(2)}) collective-permute-start(f32[4,32,10,1]{1,2,3,0:T(8,128)S(1)} %get-tuple-element.23), channel_id=1, source_target_pairs={{1,0},{2,1},{3,2},{4,3},{5,4},{6,5},{7,6},{8,7},{9,8},{10,9},{11,1... | collective-permute-start | bytes 15368 | tf_op jit(solution)/shard_map/ppermute | solution.py:18
  179.8 22.8 %all-to-all-start.1 = ((f32[4,128,128]{2,0,1:T(4,128)}), f32[4,128,128]{2,0,1:T(4,128)S(1)}, u32[]{:S(2)}, u32[]{:S(2)}) async-start(f32[4,128,128]{2,0,1:T(4,128)} %copy.212), calls=%async_computation.1 | async-start | bytes 524288 | tf_op jit(solution)/shard_map/all_to_all | solution.py:59
  316.9 5.6 collective-permute-start.5
  326.7 6.1 collective-permute-start.6
  341.1 7.6 collective-permute-start.9
  343.1 6.9 collective-permute-start.8
  352.9 6.1 collective-permute-start.10
  366.3 7.6 collective-permute-start.13
  368.2 7.0 collective-permute-start.12
  378.1 7.3 collective-permute-start.14
  468.3 24.7 %all-to-all-start.2 = ((f32[4,128,128]{2,0,1:T(4,128)}), f32[4,128,128]{2,0,1:T(4,128)S(1)}, u32[]{:S(2)}, u32[]{:S(2)}) async-start(f32[4,128,128]{2,0,1:T(4,128)} %copy.244), calls=%async_computation.2 | async-start | bytes 524288 | tf_op jit(solution)/shard_map/all_to_all | solution.py:55
  481.5 5.9 collective-permute-start.17
  566.0 20.0 %all-to-all-start.3 = ((f32[4,128,128]{2,0,1:T(4,128)}), f32[4,128,128]{2,0,1:T(4,128)S(1)}, u32[]{:S(2)}, u32[]{:S(2)}) async-start(f32[4,128,128]{2,0,1:T(4,128)} %copy.248), calls=%async_computation.3 | async-start | bytes 524288 | tf_op jit(solution)/shard_map/all_to_all | solution.py:59
  574.1 5.0 collective-permute-start.18
  699.1 6.4 collective-permute-start.21
  721.7 7.5 collective-permute-start.25
  724.0 6.5 collective-permute-start.24
  733.2 6.4 collective-permute-start.26
  746.9 7.4 collective-permute-start.29
  748.9 6.7 collective-permute-start.28
  758.3 5.5 collective-permute-start.30
  (52 other events, 441.0 us)
where the time goes:
time: 785 us; the launch traced here: 773 us
  local copies, waits for them, and re-layouts  379 us (48%)
  other arithmetic  222 us (28%)
  starting transfers between devices  136 us (17%)
  waiting for transfers between devices  33.4 us (4%)
    scatter-add x2, other arithmetic, on_device(): jnp.zeros_like(flat_state).at[:, cell_index].add(arrived)  189 us
    gather x2, local copies, waits for them, and re-layouts, on_device(): outgoing = flat_state[:, cell_index].reshape(channels, devices, capacity)  121 us
    gather x2, local copies, waits for them, and re-layouts, on_device(): seg_rows = incoming[:, positions].reshape(channels, well_count, seg_count)  62.5 us
    ppermute x16, starting transfers between devices, extended(): lax.ppermute(lax.slice_in_dim(block, block.shape[dim] - width, None, axis...  61.5 us
    scatter x2, local copies, waits for them, and re-layouts, on_device(): returned = jnp.zeros((channels, devices * capacity), jnp.float32).at[:, p...  49.8 us
    unnamed x99, local copies, waits for them, and re-layouts  31.5 us
    ppermute x16, starting transfers between devices, extended(): lax.ppermute(lax.slice_in_dim(block, 0, width, axis=dim), axis, backward)  31.1 us
    all_to_all x2, starting transfers between devices, to_owners(): lax.all_to_all(buffer, ('gx', 'gy'), split_axis=1, concat_axis=1, tiled=T...  24.7 us
  transfers between devices with their start and end apart: 36, of which 16 were waited for; matrix products, arithmetic and copies ran while one was open for 13% of the time, Pallas kernels for 0%

commit v1 on v0

v1 whole, which is shorter than its diff:
```python
import functools

import jax
import jax.numpy as jnp
from jax import lax
from jax.experimental import pallas as pl
from jax.experimental.pallas import tpu as pltpu
from jax.sharding import PartitionSpec as P

NEWTON = 2
SWEEPS = 4
GROUPS = 4
STEP = 8
F32 = jnp.float32
BF16 = jnp.bfloat16
MESH = pl.DeviceIdType.MESH


def halves(x):
    high = x.astype(BF16)
    return high, (x - high.astype(F32)).astype(BF16)


def onehot(size, index):
    rows = lax.broadcasted_iota(jnp.int32, (size, index.shape[1]), 0)
    return jnp.where(rows == index, 1.0, 0.0).astype(BF16)


def kernel(
    n_gx, n_gy, layers, wells,
    state_in, right, rock, table, cells, slots, inverse,
    state_out, rates_out,
    coeff, forcing, factor, corr, split, send1, recv1, split2, rows, send2, recv2, total3, total4, decay,
    xs, xr, ys, yr,
    send1_sem, recv1_sem, send2_sem, recv2_sem, rim_send, rim_recv,
):
    gx, gy = lax.axis_index("gx"), lax.axis_index("gy")
    devices = n_gx * n_gy
    me = gx * n_gy + gy
    cell_rows = layers * 8
    tiles = 4 * layers
    group = devices // GROUPS
    my_group = lax.div(me, group)

    def place(device):
        return (lax.div(device, n_gy), lax.rem(device, n_gy))

    barrier = pltpu.get_barrier_semaphore()

    def greet(step, carry):
        pl.semaphore_signal(
            barrier, inc=1, device_id=place(lax.rem(me + step, devices)), device_id_type=MESH
        )
        return carry

    lax.fori_loop(1, devices, greet, 0)

    for c in range(4):
        value = jnp.full((cell_rows, 128), 6.0, F32)
        for kind in range(8):
            value = value + jnp.where(rock[...] == kind, table[c, kind], 0.0)
        coeff[c * cell_rows : (c + 1) * cell_rows, :] = value
    state_out[...] = state_in[...]
    first = lax.broadcasted_iota(jnp.int32, decay.shape, 0)
    second = lax.broadcasted_iota(jnp.int32, decay.shape, 1)
    gap = (second - first).astype(F32)
    decay[...] = jnp.where(
        gap >= 0, 0.3 * jnp.exp(jnp.maximum(gap, 0.0) * -0.10536051565782628), 0.0
    )
    pl.semaphore_wait(barrier, devices - 1)

    lane = lax.broadcasted_iota(jnp.int32, (8, 128), 1)
    sub = lax.broadcasted_iota(jnp.int32, (8, 128), 0)

    def rim_copies(turn):
        right_x = (lax.rem(gx + 1, n_gx), gy)
        left_x = (lax.rem(gx + n_gx - 1, n_gx), gy)
        right_y = (gx, lax.rem(gy + 1, n_gy))
        left_y = (gx, lax.rem(gy + n_gy - 1, n_gy))
        plan = ((xs, xr, 1, 0, right_x), (xs, xr, 0, 1, left_x), (ys, yr, 1, 0, right_y), (ys, yr, 0, 1, left_y))
        return [
            pltpu.make_async_remote_copy(
                src_ref=src.at[turn, out_side],
                dst_ref=dst.at[turn, in_side],
                send_sem=rim_send.at[turn, k],
                recv_sem=rim_recv.at[turn, k],
                device_id=target,
                device_id_type=MESH,
            )
            for k, (src, dst, out_side, in_side, target) in enumerate(plan)
        ]

    def pack_lanes(i, value, packed):
        low, high = packed
        low = jnp.where(lane == i, pltpu.roll(value, i, axis=1), low)
        high = jnp.where(lane == i, pltpu.roll(value, lax.rem(i + 1, 128), axis=1), high)
        return low, high

    def send_rims(turn, field, packed):
        xs[turn, 0] = field[pl.ds(0, tiles, stride=8), :]
        xs[turn, 1] = field[pl.ds(7, tiles, stride=8), :]
        ys[turn, 0] = packed[0]
        ys[turn, 1] = packed[1]
        for copy in rim_copies(turn):
            copy.start()

    def wait_rims(turn):
        for copy in rim_copies(turn):
            copy.wait()

    def mask_rims(turn):
        for side, edge_x, edge_y in ((0, 0, 0), (1, n_gx - 1, n_gy - 1)):
            xr[turn, side] = jnp.where(gx == edge_x, 0.0, xr[turn, side])
            yr[turn, side] = jnp.where(gy == edge_y, 0.0, yr[turn, side])

    zero_packed = (jnp.zeros((8, 128), F32), jnp.zeros((8, 128), F32))

    def tile_at(field, i):
        return field[pl.ds(pl.multiple_of(i * 8, 8), 8), :]

    def neighbours(turn, field, i):
        value = tile_at(field, i)
        layer = lax.rem(i, layers)
        above = tile_at(field, jnp.maximum(i - 1, 0))
        below = tile_at(field, jnp.minimum(i + 1, tiles - 1))
        total = jnp.where(layer > 0, above, 0.0) + jnp.where(layer < layers - 1, below, 0.0)
        x_low = jnp.broadcast_to(xr[turn, 0, pl.ds(i, 1), :], (8, 128))
        x_high = jnp.broadcast_to(xr[turn, 1, pl.ds(i, 1), :], (8, 128))
        total = total + jnp.where(sub == 0, x_low, pltpu.roll(value, 1, axis=0))
        total = total + jnp.where(sub == 7, x_high, pltpu.roll(value, 7, axis=0))
        y_low = pltpu.roll(yr[turn, 0], lax.rem(128 - i, 128), axis=1)
        y_high = pltpu.roll(yr[turn, 1], 127 - i, axis=1)
        total = total + jnp.where(lane == 0, y_low, pltpu.roll(value, 1, axis=1))
        return value, total + jnp.where(lane == 127, y_high, pltpu.roll(value, 127, axis=1))

    def block_copy(source, target, source_slot, target_slot, device, send_sem, recv_sem):
        return pltpu.make_async_remote_copy(
            src_ref=source.at[source_slot],
            dst_ref=target.at[target_slot],
            send_sem=send_sem,
            recv_sem=recv_sem,
            device_id=place(device),
            device_id_type=MESH,
        )

    def newton(n, carry):
        turn = n * SWEEPS

        def pack_state(i, packed):
            return pack_lanes(i, tile_at(state_out, i), packed)

        send_rims(turn, state_out, lax.fori_loop(0, tiles, pack_state, zero_packed, unroll=4))

        for c in range(4):
            high, low = halves(state_out[c * cell_rows : (c + 1) * cell_rows, :])
            split[c, :, 0:128] = high
            split[c, :, 128:256] = low

        def gather_pair(pair):
            index = jnp.concatenate([cells[pl.ds(2 * pair + k, 1), :] for k in range(2)], axis=1)
            pick = onehot(128, index & 127)
            pick = jnp.concatenate([pick, pick], axis=0)
            wanted = lax.broadcasted_iota(jnp.int32, (cell_rows, 256), 0) == (index >> 7)
            found = []
            for c in range(4):
                value = jnp.dot(split[c], pick, preferred_element_type=F32)
                found.append(jnp.sum(jnp.where(wanted, value, 0.0), axis=0, keepdims=True))
            found = jnp.concatenate(found, axis=0)
            return found[:, :128], found[:, 128:]

        my_pair = lax.div(me, 2)
        pairs = devices // 2

        def gather_step(step, inner):
            pair = lax.rem(my_pair + 1 + step, pairs)
            for k, block in enumerate(gather_pair(pair)):
                send1[n, 2 * pair + k] = block
                block_copy(
                    send1.at[n], recv1.at[n], 2 * pair + k, me, 2 * pair + k, send1_sem.at[n], recv1_sem.at[n]
                ).start()
            return inner

        lax.fori_loop(0, pairs - 1, gather_step, 0)
        for k, block in enumerate(gather_pair(my_pair)):
            send1[n, 2 * my_pair + k] = block
        partner = 4 * my_pair + 1 - me
        block_copy(
            send1.at[n], recv1.at[n], partner, me, partner, send1_sem.at[n], recv1_sem.at[n]
        ).start()
        recv1[n, me] = send1[n, me]

        wait_rims(turn)
        mask_rims(turn)

        def base(i, inner):
            value, near = neighbours(turn, state_out, i)
            at = pl.ds(pl.multiple_of(i * 8, 8), 8)
            square = value * value
            forcing[at, :] = coeff[at, :] * value - near + 0.1 * square * value - right[at, :]
            factor[at, :] = 1.0 / (coeff[at, :] + 0.3 * square)
            return inner

        lax.fori_loop(0, tiles, base, 0, unroll=4)

        all_blocks = pl.ds(0, devices - 1)
        arrived = pltpu.make_async_remote_copy(
            src_ref=send1.at[n, all_blocks],
            dst_ref=recv1.at[n, all_blocks],
            send_sem=send1_sem.at[n],
            recv_sem=recv1_sem.at[n],
            device_id=place(me),
            device_id_type=MESH,
        )
        arrived.wait_recv()

        high, low = halves(recv1[n].reshape(4 * devices, 128))
        split2[:, 0:128] = high
        split2[:, 128:256] = low
        quarter = lax.broadcasted_iota(jnp.int32, (4 * devices, 256), 0) >> 2

        def owner_gather(w, inner):
            index = slots[pl.ds(w, 1), :]
            pick = onehot(128, index & 127)
            pick = jnp.concatenate([pick, pick], axis=0)
            value = jnp.dot(split2[...], pick, preferred_element_type=F32)
            value = jnp.where(quarter == (index >> 7), value, 0.0)
            value = jnp.sum(value.reshape(devices // 2, 8, 256), axis=0)
            value = value[0:4] + value[4:8]
            rows[0, pl.ds(w, 4, stride=wells), :] = value[:, :128]
            rows[1, pl.ds(w, 4, stride=wells), :] = value[:, 128:]
            return inner

        lax.fori_loop(0, wells, owner_gather, 0)
        flows = []
        for i in range(4):
            sides = []
            for half in range(2):
                at = slice(half * 128, half * 128 + 128)
                flow = inverse[i, 0, :, at] * rows[half, 0:wells, :]
                for j in range(1, 4):
                    flow = flow + inverse[i, j, :, at] * rows[half, j * wells : (j + 1) * wells, :]
                sides.append(flow)
            flows.append(jnp.concatenate(sides, axis=1))
        rates = jnp.dot(
            jnp.concatenate(flows, axis=0),
            decay[...],
            precision=lax.Precision.HIGHEST,
            preferred_element_type=F32,
        )
        rates_out[...] = rates
        rows[0] = rates[:, :128]
        rows[1] = rates[:, 128:]
        total3[...] = jnp.zeros_like(total3)

        def owner_scatter(w, inner):
            index = slots[pl.ds(w, 1), :]
            pick = onehot(128, index & 127)
            rate = jnp.concatenate([rows[k, pl.ds(w, 4, stride=wells), :] for k in range(2)], axis=1)
            rate = jnp.concatenate([rate, rate], axis=0)
            wanted = quarter == (index >> 7)
            parts = []
            for half in halves(rate):
                spread = jnp.broadcast_to(half.astype(F32)[None], (devices // 2, 8, 256))
                spread = spread.reshape(4 * devices, 256)
                parts.append(jnp.where(wanted, spread, 0.0).astype(BF16))
            total3[...] += lax.dot_general(
                jnp.concatenate(parts, axis=1),
                jnp.concatenate([pick, pick], axis=1),
                (((1,), (1,)), ((), ())),
                preferred_element_type=F32,
            )
            return inner

        lax.fori_loop(0, wells, owner_scatter, 0)
        send2[n] = total3[...].reshape(devices, 4, 128)
        recv2[n, me] = send2[n, me]

        def return_step(step, inner):
            j = lax.div(step, group)
            target = lax.rem(my_group + j, GROUPS) * group + lax.rem(me + step, group)
            block_copy(
                send2.at[n], recv2.at[n], target, me, target, send2_sem.at[n], recv2_sem.at[n, j]
            ).start()
            return inner

        lax.fori_loop(1, devices, return_step, 0)
        arrived.wait_send()

        total4[...] = jnp.zeros_like(total4)

        def wait_group(j, count):
            some = pl.ds(0, count)
            pltpu.make_async_remote_copy(
                src_ref=send2.at[n, some],
                dst_ref=recv2.at[n, some],
                send_sem=send2_sem.at[n],
                recv_sem=recv2_sem.at[n, j],
                device_id=place(me),
                device_id_type=MESH,
            ).wait_recv()

        def inflow_group(j):
            start = lax.rem(my_group + GROUPS - j, GROUPS) * group

            def inflow_step(step, inner):
                owner = start + step * STEP
                index = jnp.concatenate([cells[pl.ds(owner + k, 1), :] for k in range(STEP)], axis=1)
                value = jnp.concatenate([recv2[n, owner + k] for k in range(STEP)], axis=1)
                lanes = onehot(128, index & 127)
                pick = onehot(cell_rows, index >> 7)
                pick = jnp.concatenate([pick, pick], axis=1)
                high, low = halves(value)
                for c in range(4):
                    spread = jnp.concatenate([lanes * high[c : c + 1], lanes * low[c : c + 1]], axis=1)
                    total4[c] += lax.dot_general(
                        spread, pick, (((1,), (1,)), ((), ())), preferred_element_type=F32
                    )
                return inner

            lax.fori_loop(0, group // STEP, inflow_step, 0)

        wait_group(0, group - 1)
        inflow_group(0)
        for j in range(1, GROUPS):
            wait_group(j, group)
            inflow_group(j)
        sent = pl.ds(0, devices - 1)
        pltpu.make_async_remote_copy(
            src_ref=send2.at[n, sent],
            dst_ref=recv2.at[n, sent],
            send_sem=send2_sem.at[n],
            recv_sem=recv2_sem.at[n, 0],
            device_id=place(me),
            device_id_type=MESH,
        ).wait_send()

        for c in range(4):
            at = slice(c * cell_rows, (c + 1) * cell_rows)
            forcing[at, :] = forcing[at, :] - total4[c].T

        def first_sweep(i, packed):
            at = pl.ds(pl.multiple_of(i * 8, 8), 8)
            value = forcing[at, :] * factor[at, :]
            corr[0, at, :] = value
            return pack_lanes(i, value, packed)

        packed = lax.fori_loop(0, tiles, first_sweep, zero_packed, unroll=4)
        for k in range(1, SWEEPS):
            now, later = corr.at[(k - 1) % 2], corr.at[k % 2]
            send_rims(turn + k, now, packed)
            wait_rims(turn + k)
            mask_rims(turn + k)

            def sweep(i, packed):
                at = pl.ds(pl.multiple_of(i * 8, 8), 8)
                _, near = neighbours(turn + k, now, i)
                value = (forcing[at, :] + near) * factor[at, :]
                if k == SWEEPS - 1:
                    state_out[at, :] = state_out[at, :] - value
                    return packed
                later[at, :] = value
                return pack_lanes(i, value, packed)

            packed = lax.fori_loop(0, tiles, sweep, zero_packed, unroll=4)
        return carry

    lax.fori_loop(0, NEWTON, newton, 0)


def on_device(n_gx, n_gy, state_init, right_side, rock_type, trans_table, perf_cells, seg_slot, seg_inverse):
    channels, layers, rows, columns = state_init.shape
    devices = n_gx * n_gy
    wells, segments = seg_slot.shape
    cell_rows = layers * rows
    tiles = channels * layers
    field = (channels * cell_rows, columns)
    vmem = pl.BlockSpec(memory_space=pltpu.VMEM)
    smem = pl.BlockSpec(memory_space=pltpu.SMEM)
    turns = NEWTON * SWEEPS
    dma = pltpu.SemaphoreType.DMA
    state, rates = pl.pallas_call(
        functools.partial(kernel, n_gx, n_gy, layers, wells),
        out_shape=(
            jax.ShapeDtypeStruct(field, F32),
            jax.ShapeDtypeStruct((channels * wells, segments), F32),
        ),
        in_specs=[vmem, vmem, vmem, smem, vmem, vmem, vmem],
        out_specs=(vmem, vmem),
        scratch_shapes=[
            pltpu.VMEM(field, F32),
            pltpu.VMEM(field, F32),
            pltpu.VMEM(field, F32),
            pltpu.VMEM((2,) + field, F32),
            pltpu.VMEM((channels, cell_rows, 256), BF16),
            pltpu.VMEM((NEWTON, devices, channels, 128), F32),
            pltpu.VMEM((NEWTON, devices, channels, 128), F32),
            pltpu.VMEM((channels * devices, 256), BF16),
            pltpu.VMEM((2, channels * wells, 128), F32),
            pltpu.VMEM((NEWTON, devices, channels, 128), F32),
            pltpu.VMEM((NEWTON, devices, channels, 128), F32),
            pltpu.VMEM((channels * devices, 128), F32),
            pltpu.VMEM((channels, 128, cell_rows), F32),
            pltpu.VMEM((segments, segments), F32),
            pltpu.VMEM((turns, 2, tiles, 128), F32),
            pltpu.VMEM((turns, 2, tiles, 128), F32),
            pltpu.VMEM((turns, 2, 8, 128), F32),
            pltpu.VMEM((turns, 2, 8, 128), F32),
            dma((NEWTON,)),
            dma((NEWTON,)),
            dma((NEWTON,)),
            dma((NEWTON, GROUPS)),
            dma((turns, 4)),
            dma((turns, 4)),
        ],
        compiler_params=pltpu.CompilerParams(
            collective_id=0, has_side_effects=True, vmem_limit_bytes=48 * 1024 * 1024
        ),
        name="newton",
    )(
        state_init.reshape(field),
        right_side.reshape(field),
        rock_type.reshape(cell_rows, columns),
        trans_table,
        perf_cells.reshape(devices, perf_cells.shape[2]),
        seg_slot,
        seg_inverse,
    )
    return state.reshape(state_init.shape), rates.reshape(channels, wells, segments)


def solution(mesh):
    in_specs = (
        P(None, None, "gx", "gy"),
        P(None, None, "gx", "gy"),
        P(None, "gx", "gy"),
        P(),
        P(("gx", "gy"), None, None),
        P(("gx", "gy"), None),
        P(None, None, ("gx", "gy"), None),
    )
    out_specs = (P(None, None, "gx", "gy"), P(None, ("gx", "gy"), None))
    return jax.shard_map(
        functools.partial(on_device, mesh.shape["gx"], mesh.shape["gy"]),
        mesh=mesh,
        in_specs=in_specs,
        out_specs=out_specs,
        check_vma=False,
    )
```

time: 785 us -> 228 us (0.29); the launches traced: 773 us -> 228 us
  local copies, waits for them, and re-layouts: 379 us -> 7.75 us
  other arithmetic: 222 us -> 0 us
  Pallas kernels: 0 us -> 219 us
  starting transfers between devices: 136 us -> 0 us
  waiting for transfers between devices: 33.4 us -> 0 us
    pallas_call x0 -> x1, Pallas kernels: none -> 219 us  [on_device(): pl.pallas_call(functools.partial(kernel, n_gx, n_gy, layers, wells), out_...]
    scatter-add x2 -> x0, other arithmetic: 189 us -> none  [on_device(): jnp.zeros_like(flat_state).at[:, cell_index].add(arrived)]
    gather x4 -> x0, local copies, waits for them, and re-layouts: 184 us -> none  [the longest x2 121 us: on_device(): outgoing = flat_state[:, cell_index].reshape(channels, devices, capacity)]
    ppermute x32 -> x0, starting transfers between devices: 92.7 us -> none  [the longest x16 61.5 us: extended(): lax.ppermute(lax.slice_in_dim(block, block.shape[dim] - width, None, axis...]
    reshape x8 -> x0, local copies, waits for them, and re-layouts: 55.4 us -> none  [the longest x2 21.6 us: on_device(): jnp.zeros_like(flat_state).at[:, cell_index].add(arrived)]
    scatter x2 -> x0, local copies, waits for them, and re-layouts: 49.8 us -> none  [on_device(): returned = jnp.zeros((channels, devices * capacity), jnp.float32).at[:, p...]
    all_to_all x4 -> x0, starting transfers between devices: 43.3 us -> none  [the longest x2 24.7 us: to_owners(): lax.all_to_all(buffer, ('gx', 'gy'), split_axis=1, concat_axis=1, tiled=T...]
    ppermute x32 -> x0, waiting for transfers between devices: 29.5 us -> none  [the longest x16 20.7 us: extended(): lax.ppermute(lax.slice_in_dim(block, 0, width, axis=dim), axis, backward)]
  transfers between devices with their start and end apart: 36 -> 0, of which waited for: 16 -> 0; matrix products, arithmetic and copies ran while one was open for 13% -> 0% of each run, Pallas kernels for 0% -> 0%
where the time goes in v1:
time: 228 us
  Pallas kernels  219 us (96%)
  local copies, waits for them, and re-layouts  7.75 us (3%)
    pallas_call x1, Pallas kernels, on_device(): pl.pallas_call(functools.partial(kernel, n_gx, n_gy, layers, wells), out_...  219 us
    unnamed x16, local copies, waits for them, and re-layouts  7.75 us

profile of v1, /device:TPU:1, one launch (start us, length us, event | category | flops | bytes accessed | tf_op | source)
XLA Modules:
  0.0 227.6 jit_solution(17455567400278130070)
XLA Ops:
  0.6 0.0 copy-start.6
  0.6 0.7 copy-done.6
  1.3 0.0 copy-start
  1.3 1.0 copy-done
  2.4 0.0 copy-start.1
  2.4 1.0 copy-done.1
  3.4 0.0 copy-start.2
  3.4 1.0 copy-done.2
  4.4 0.0 copy-start.3
  4.4 0.9 copy-done.3
  5.3 0.0 copy-start.4
  5.3 0.8 copy-done.4
  6.2 0.0 copy-start.5
  6.2 0.8 copy-done.5
  6.9 219.2 %newton.1 = (f32[1024,128]{1,0:T(8,128)S(1)}, f32[128,256]{1,0:T(8,128)S(1)}) custom-call(f32[1024,128]{1,0:T(8,128)S(1)} %bitcast.7, f32[1024,128]{1,0:T(8,128)S(1)} %bitcast.8, s32[256,128]{1,0:T(8,128)S(1)} %bitcast.10, f32[4,8]{1,0:T(4,128)S(1)} %copy-done.6, s32[128,128]{1,0:T(8,128)S(1)} %bitcast.11, s32[32,256]{1,0:T(8,128)S(1)} %copy-done.5, ...), custom_call_target="tpu_custom_call" | custom-call | tf_op jit(solution)/shard_map/newton/pallas_call | solution.py:381
  226.1 0.8 copy.11
  226.9 0.7 copy.12
Async XLA Ops:
  0.6 0.7 copy-start.6
  1.3 1.0 copy-start
  2.4 1.0 copy-start.1
  3.4 1.0 copy-start.2
  4.4 0.9 copy-start.3
  5.3 0.8 copy-start.4
  6.2 0.8 copy-start.5

commit v2 on v1

--- a/solution.py
+++ b/solution.py
@@ -10,7 +10,8 @@
 NEWTON = 2
 SWEEPS = 4
 GROUPS = 4
-STEP = 8
+STEP = 16
+WELLS_STEP = 8
 F32 = jnp.float32
 BF16 = jnp.bfloat16
 MESH = pl.DeviceIdType.MESH
@@ -28,8 +29,9 @@
 
 def kernel(
     n_gx, n_gy, layers, wells,
-    state_in, right, rock, table, cells, slots, inverse,
+    state_in, right_in, rock_in, table, cells_in, slots_in, inverse_in,
     state_out, rates_out,
+    right, rock, cells, slots, inverse, load_sem,
     coeff, forcing, factor, corr, split, send1, recv1, split2, rows, send2, recv2, total3, total4, decay,
     xs, xr, ys, yr,
     send1_sem, recv1_sem, send2_sem, recv2_sem, rim_send, rim_recv,
@@ -45,6 +47,22 @@
     def place(device):
         return (lax.div(device, n_gy), lax.rem(device, n_gy))
 
+    loads = [
+        pltpu.make_async_copy(source, target, load_sem.at[k])
+        for k, (source, target) in enumerate(
+            (
+                (rock_in, rock),
+                (state_in, state_out),
+                (cells_in, cells),
+                (right_in, right),
+                (slots_in, slots),
+                (inverse_in, inverse),
+            )
+        )
+    ]
+    for load in loads:
+        load.start()
+
     barrier = pltpu.get_barrier_semaphore()
 
     def greet(step, carry):
@@ -55,18 +73,28 @@
 
     lax.fori_loop(1, devices, greet, 0)
 
-    for c in range(4):
-        value = jnp.full((cell_rows, 128), 6.0, F32)
-        for kind in range(8):
-            value = value + jnp.where(rock[...] == kind, table[c, kind], 0.0)
-        coeff[c * cell_rows : (c + 1) * cell_rows, :] = value
-    state_out[...] = state_in[...]
+    loads[0].wait()
+
+    def coefficients(i, inner):
+        at = pl.ds(pl.multiple_of(i * 8, 8), 8)
+        kinds = rock[at, :]
+        picked = [kinds == kind for kind in range(8)]
+        for c in range(4):
+            value = jnp.full((8, 128), 6.0, F32)
+            for kind in range(8):
+                value = value + jnp.where(picked[kind], table[c, kind], 0.0)
+            coeff[pl.ds(pl.multiple_of(c * cell_rows + i * 8, 8), 8), :] = value
+        return inner
+
+    lax.fori_loop(0, layers, coefficients, 0, unroll=2)
     first = lax.broadcasted_iota(jnp.int32, decay.shape, 0)
     second = lax.broadcasted_iota(jnp.int32, decay.shape, 1)
     gap = (second - first).astype(F32)
     decay[...] = jnp.where(
         gap >= 0, 0.3 * jnp.exp(jnp.maximum(gap, 0.0) * -0.10536051565782628), 0.0
     )
+    for load in loads[1:]:
+        load.wait()
     pl.semaphore_wait(barrier, devices - 1)
 
     lane = lax.broadcasted_iota(jnp.int32, (8, 128), 1)
@@ -90,11 +118,24 @@
             for k, (src, dst, out_side, in_side, target) in enumerate(plan)
         ]
 
-    def pack_lanes(i, value, packed):
-        low, high = packed
-        low = jnp.where(lane == i, pltpu.roll(value, i, axis=1), low)
-        high = jnp.where(lane == i, pltpu.roll(value, lax.rem(i + 1, 128), axis=1), high)
-        return low, high
+    def for_tiles(body):
+        def channel(c, packed):
+            low, high = jnp.zeros((8, 128), F32), jnp.zeros((8, 128), F32)
+            edge = None
+            for z in range(layers):
+                at = pl.ds(pl.multiple_of(c * cell_rows + z * 8, 8), 8)
+                edge = body(c, z, at)
+                if edge is not None:
+                    low = jnp.where(lane == z, pltpu.roll(edge, z, axis=1) if z else edge, low)
+                    high = jnp.where(lane == z, pltpu.roll(edge, z + 1, axis=1), high)
+            if edge is None:
+                return packed
+            ours = (lane >= c * layers) & (lane < (c + 1) * layers)
+            low = jnp.where(ours, pltpu.roll(low, c * layers, axis=1), packed[0])
+            high = jnp.where(ours, pltpu.roll(high, c * layers, axis=1), packed[1])
+            return low, high
+
+        return lax.fori_loop(0, 4, channel, zero_packed)
 
     def send_rims(turn, field, packed):
         xs[turn, 0] = field[pl.ds(0, tiles, stride=8), :]
@@ -115,23 +156,22 @@
 
     zero_packed = (jnp.zeros((8, 128), F32), jnp.zeros((8, 128), F32))
 
-    def tile_at(field, i):
-        return field[pl.ds(pl.multiple_of(i * 8, 8), 8), :]
-
-    def neighbours(turn, field, i):
-        value = tile_at(field, i)
-        layer = lax.rem(i, layers)
-        above = tile_at(field, jnp.maximum(i - 1, 0))
-        below = tile_at(field, jnp.minimum(i + 1, tiles - 1))
-        total = jnp.where(layer > 0, above, 0.0) + jnp.where(layer < layers - 1, below, 0.0)
-        x_low = jnp.broadcast_to(xr[turn, 0, pl.ds(i, 1), :], (8, 128))
-        x_high = jnp.broadcast_to(xr[turn, 1, pl.ds(i, 1), :], (8, 128))
-        total = total + jnp.where(sub == 0, x_low, pltpu.roll(value, 1, axis=0))
-        total = total + jnp.where(sub == 7, x_high, pltpu.roll(value, 7, axis=0))
-        y_low = pltpu.roll(yr[turn, 0], lax.rem(128 - i, 128), axis=1)
-        y_high = pltpu.roll(yr[turn, 1], 127 - i, axis=1)
+    def neighbours(turn, field, c, z, at):
+        value = field[at, :]
+        row = c * layers + z
+        y_low = pltpu.roll(yr[turn, 0], lax.rem(128 - row, 128), axis=1)
+        y_high = pltpu.roll(yr[turn, 1], 127 - row, axis=1)
+        total = jnp.where(sub == 0, jnp.broadcast_to(xr[turn, 0, pl.ds(row, 1), :], (8, 128)), pltpu.roll(value, 1, axis=0))
+        total = total + jnp.where(
+            sub == 7, jnp.broadcast_to(xr[turn, 1, pl.ds(row, 1), :], (8, 128)), pltpu.roll(value, 7, axis=0)
+        )
         total = total + jnp.where(lane == 0, y_low, pltpu.roll(value, 1, axis=1))
-        return value, total + jnp.where(lane == 127, y_high, pltpu.roll(value, 127, axis=1))
+        total = total + jnp.where(lane == 127, y_high, pltpu.roll(value, 127, axis=1))
+        if z > 0:
+            total = total + field[pl.ds(pl.multiple_of(c * cell_rows + z * 8 - 8, 8), 8), :]
+        if z < layers - 1:
+            total = total + field[pl.ds(pl.multiple_of(c * cell_rows + z * 8 + 8, 8), 8), :]
+        return value, total
 
     def block_copy(source, target, source_slot, target_slot, device, send_sem, recv_sem):
         return pltpu.make_async_remote_copy(
@@ -146,10 +186,7 @@
     def newton(n, carry):
         turn = n * SWEEPS
 
-        def pack_state(i, packed):
-            return pack_lanes(i, tile_at(state_out, i), packed)
-
-        send_rims(turn, state_out, lax.fori_loop(0, tiles, pack_state, zero_packed, unroll=4))
+        send_rims(turn, state_out, for_tiles(lambda c, z, at: state_out[at, :]))
 
         for c in range(4):
             high, low = halves(state_out[c * cell_rows : (c + 1) * cell_rows, :])
@@ -180,7 +217,7 @@
                 ).start()
             return inner
 
-        lax.fori_loop(0, pairs - 1, gather_step, 0)
+        lax.fori_loop(0, pairs - 1, gather_step, 0, unroll=7)
         for k, block in enumerate(gather_pair(my_pair)):
             send1[n, 2 * my_pair + k] = block
         partner = 4 * my_pair + 1 - me
@@ -192,15 +229,13 @@
         wait_rims(turn)
         mask_rims(turn)
 
-        def base(i, inner):
-            value, near = neighbours(turn, state_out, i)
-            at = pl.ds(pl.multiple_of(i * 8, 8), 8)
+        def base(c, z, at):
+            value, near = neighbours(turn, state_out, c, z, at)
             square = value * value
             forcing[at, :] = coeff[at, :] * value - near + 0.1 * square * value - right[at, :]
             factor[at, :] = 1.0 / (coeff[at, :] + 0.3 * square)
-            return inner
-
-        lax.fori_loop(0, tiles, base, 0, unroll=4)
+
+        for_tiles(base)
 
         all_blocks = pl.ds(0, devices - 1)
         arrived = pltpu.make_async_remote_copy(
@@ -230,7 +265,7 @@
             rows[1, pl.ds(w, 4, stride=wells), :] = value[:, 128:]
             return inner
 
-        lax.fori_loop(0, wells, owner_gather, 0)
+        lax.fori_loop(0, wells, owner_gather, 0, unroll=4)
         flows = []
         for i in range(4):
             sides = []
@@ -252,17 +287,20 @@
         rows[1] = rates[:, 128:]
         total3[...] = jnp.zeros_like(total3)
 
-        def owner_scatter(w, inner):
-            index = slots[pl.ds(w, 1), :]
+        def owner_scatter(step, inner):
+            first_well = step * WELLS_STEP
+            width = WELLS_STEP * 256
+            index = jnp.concatenate([slots[pl.ds(first_well + k, 1), :] for k in range(WELLS_STEP)], axis=1)
+            rate = jnp.concatenate(
+                [rows[half, pl.ds(first_well + k, 4, stride=wells), :] for k in range(WELLS_STEP) for half in range(2)],
+                axis=1,
+            )
             pick = onehot(128, index & 127)
-            rate = jnp.concatenate([rows[k, pl.ds(w, 4, stride=wells), :] for k in range(2)], axis=1)
-            rate = jnp.concatenate([rate, rate], axis=0)
-            wanted = quarter == (index >> 7)
+            wanted = (lax.broadcasted_iota(jnp.int32, (4 * devices, width), 0) >> 2) == (index >> 7)
             parts = []
-            for half in halves(rate):
-                spread = jnp.broadcast_to(half.astype(F32)[None], (devices // 2, 8, 256))
-                spread = spread.reshape(4 * devices, 256)
-                parts.append(jnp.where(wanted, spread, 0.0).astype(BF16))
+            for half in halves(jnp.concatenate([rate, rate], axis=0)):
+                spread = jnp.broadcast_to(half.astype(F32)[None], (devices // 2, 8, width))
+                parts.append(jnp.where(wanted, spread.reshape(4 * devices, width), 0.0).astype(BF16))
             total3[...] += lax.dot_general(
                 jnp.concatenate(parts, axis=1),
                 jnp.concatenate([pick, pick], axis=1),
@@ -271,7 +309,7 @@
             )
             return inner
 
-        lax.fori_loop(0, wells, owner_scatter, 0)
+        lax.fori_loop(0, wells // WELLS_STEP, owner_scatter, 0)
         send2[n] = total3[...].reshape(devices, 4, 128)
         recv2[n, me] = send2[n, me]
 
@@ -310,11 +348,16 @@
                 pick = onehot(cell_rows, index >> 7)
                 pick = jnp.concatenate([pick, pick], axis=1)
                 high, low = halves(value)
-                for c in range(4):
-                    spread = jnp.concatenate([lanes * high[c : c + 1], lanes * low[c : c + 1]], axis=1)
-                    total4[c] += lax.dot_general(
-                        spread, pick, (((1,), (1,)), ((), ())), preferred_element_type=F32
-                    )
+                spread = jnp.concatenate(
+                    [
+                        jnp.concatenate([lanes * high[c : c + 1], lanes * low[c : c + 1]], axis=1)
+                        for c in range(4)
+                    ],
+                    axis=0,
+                )
+                total4[...] += lax.dot_general(
+                    pick, spread, (((1,), (1,)), ((), ())), preferred_element_type=F32
+                )
                 return inner
 
             lax.fori_loop(0, group // STEP, inflow_step, 0)
@@ -336,32 +379,29 @@
 
         for c in range(4):
             at = slice(c * cell_rows, (c + 1) * cell_rows)
-            forcing[at, :] = forcing[at, :] - total4[c].T
-
-        def first_sweep(i, packed):
-            at = pl.ds(pl.multiple_of(i * 8, 8), 8)
+            forcing[at, :] = forcing[at, :] - total4[:, c * 128 : (c + 1) * 128]
+
+        def first_sweep(c, z, at):
             value = forcing[at, :] * factor[at, :]
             corr[0, at, :] = value
-            return pack_lanes(i, value, packed)
-
-        packed = lax.fori_loop(0, tiles, first_sweep, zero_packed, unroll=4)
+            return value
+
+        packed = for_tiles(first_sweep)
         for k in range(1, SWEEPS):
             now, later = corr.at[(k - 1) % 2], corr.at[k % 2]
             send_rims(turn + k, now, packed)
             wait_rims(turn + k)
             mask_rims(turn + k)
 
-            def sweep(i, packed):
-                at = pl.ds(pl.multiple_of(i * 8, 8), 8)
-                _, near = neighbours(turn + k, now, i)
+            def sweep(c, z, at):
+                _, near = neighbours(turn + k, now, c, z, at)
                 value = (forcing[at, :] + near) * factor[at, :]
-                if k == SWEEPS - 1:
-                    state_out[at, :] = state_out[at, :] - value
-                    return packed
-                later[at, :] = value
-                return pack_lanes(i, value, packed)
-
-            packed = lax.fori_loop(0, tiles, sweep, zero_packed, unroll=4)
+                if k < SWEEPS - 1:
+                    later[at, :] = value
+                    return value
+                state_out[at, :] = state_out[at, :] - value
+
+            packed = for_tiles(sweep)
         return carry
 
     lax.fori_loop(0, NEWTON, newton, 0)
@@ -375,6 +415,7 @@
     tiles = channels * layers
     field = (channels * cell_rows, columns)
     vmem = pl.BlockSpec(memory_space=pltpu.VMEM)
+    hbm = pl.BlockSpec(memory_space=pl.ANY)
     smem = pl.BlockSpec(memory_space=pltpu.SMEM)
     turns = NEWTON * SWEEPS
     dma = pltpu.SemaphoreType.DMA
@@ -384,9 +425,15 @@
             jax.ShapeDtypeStruct(field, F32),
             jax.ShapeDtypeStruct((channels * wells, segments), F32),
         ),
-        in_specs=[vmem, vmem, vmem, smem, vmem, vmem, vmem],
+        in_specs=[hbm, hbm, hbm, smem, hbm, hbm, hbm],
         out_specs=(vmem, vmem),
         scratch_shapes=[
+            pltpu.VMEM(field, F32),
+            pltpu.VMEM((cell_rows, columns), jnp.int32),
+            pltpu.VMEM((devices, perf_cells.shape[2]), jnp.int32),
+            pltpu.VMEM((wells, segments), jnp.int32),
+            pltpu.VMEM(seg_inverse.shape, F32),
+            dma((6,)),
             pltpu.VMEM(field, F32),
             pltpu.VMEM(field, F32),
             pltpu.VMEM(field, F32),
@@ -399,7 +446,7 @@
             pltpu.VMEM((NEWTON, devices, channels, 128), F32),
             pltpu.VMEM((NEWTON, devices, channels, 128), F32),
             pltpu.VMEM((channels * devices, 128), F32),
-            pltpu.VMEM((channels, 128, cell_rows), F32),
+            pltpu.VMEM((cell_rows, channels * 128), F32),
             pltpu.VMEM((segments, segments), F32),
             pltpu.VMEM((turns, 2, tiles, 128), F32),
             pltpu.VMEM((turns, 2, tiles, 128), F32),
@@ -413,7 +460,7 @@
             dma((turns, 4)),
         ],
         compiler_params=pltpu.CompilerParams(
-            collective_id=0, has_side_effects=True, vmem_limit_bytes=48 * 1024 * 1024
+            collective_id=0, has_side_effects=True, vmem_limit_bytes=62 * 1024 * 1024
         ),
         name="newton",
     )(

time: 228 us -> 150 us (0.66)
  Pallas kernels: 219 us -> 146 us
  local copies, waits for them, and re-layouts: 7.75 us -> 2.56 us
    pallas_call x1, Pallas kernels: 219 us -> 146 us  [on_device(): pl.pallas_call(functools.partial(kernel, n_gx, n_gy, layers, wells), out_...]
    unnamed x16 -> x4, local copies, waits for them, and re-layouts: 7.75 us -> 2.56 us
where the time goes in v2:
time: 150 us; the launch traced here: 149 us
  Pallas kernels  146 us (97%)
  local copies, waits for them, and re-layouts  2.56 us (2%)
    pallas_call x1, Pallas kernels, on_device(): pl.pallas_call(functools.partial(kernel, n_gx, n_gy, layers, wells), out_...  146 us

profile of v2, /device:TPU:1, one launch (start us, length us, event | category | flops | bytes accessed | tf_op | source)
XLA Modules:
  0.0 149.5 jit_solution(5484971084920367180)
XLA Ops:
  0.6 146.2 %newton.1 = (f32[1024,128]{1,0:T(8,128)}, f32[128,256]{1,0:T(8,128)}) custom-call(f32[1024,128]{1,0:T(8,128)} %bitcast.7, f32[1024,128]{1,0:T(8,128)} %bitcast.8, s32[256,128]{1,0:T(8,128)} %bitcast.10, f32[4,8]{1,0:T(4,128)} %table.1, s32[128,128]{1,0:T(8,128)} %bitcast.11, s32[32,256]{1,0:T(8,128)} %slots_in.1, f32[4,4,32,256]{3,2,1,0:T(8,128)} %inverse_in.1), custom_call_target="tpu_custom_call" | custom-call | tf_op jit(solution)/shard_map/newton/pallas_call | solution.py:422
  146.9 0.0 copy-start
  146.9 1.9 %copy.11 = f32[4,32,8,128]{3,2,1,0:T(8,128)} copy(f32[4,32,8,128]{3,2,1,0:T(8,128)} %bitcast.6) | data formatting | bytes 1048576
  148.8 0.0 copy-done
  148.8 0.7 copy.12
Async XLA Ops:
  146.9 1.9 %copy-start = (f32[128,256]{1,0:T(8,128)S(1)}, f32[128,256]{1,0:T(8,128)}, u32[]{:S(2)}) copy-start(f32[128,256]{1,0:T(8,128)} %get-tuple-element.5) | copy-start | bytes 393220

commit v3 on v2

--- a/solution.py
+++ b/solution.py
@@ -9,9 +9,10 @@
 
 NEWTON = 2
 SWEEPS = 4
-GROUPS = 4
+GROUPS = 2
 STEP = 16
 WELLS_STEP = 8
+CHUNK = 4
 F32 = jnp.float32
 BF16 = jnp.bfloat16
 MESH = pl.DeviceIdType.MESH
@@ -95,83 +96,86 @@
     )
     for load in loads[1:]:
         load.wait()
-    pl.semaphore_wait(barrier, devices - 1)
 
     lane = lax.broadcasted_iota(jnp.int32, (8, 128), 1)
     sub = lax.broadcasted_iota(jnp.int32, (8, 128), 0)
 
-    def rim_copies(turn):
+    def rim_copies(turn, c):
         right_x = (lax.rem(gx + 1, n_gx), gy)
         left_x = (lax.rem(gx + n_gx - 1, n_gx), gy)
         right_y = (gx, lax.rem(gy + 1, n_gy))
         left_y = (gx, lax.rem(gy + n_gy - 1, n_gy))
-        plan = ((xs, xr, 1, 0, right_x), (xs, xr, 0, 1, left_x), (ys, yr, 1, 0, right_y), (ys, yr, 0, 1, left_y))
+        mine = pl.ds(pl.multiple_of(c * layers, layers), layers)
+        plan = (
+            (xs.at[turn, 1, mine], xr.at[turn, 0, mine], right_x),
+            (xs.at[turn, 0, mine], xr.at[turn, 1, mine], left_x),
+            (ys.at[turn, c], yr.at[turn, c, 0], right_y),
+            (ys.at[turn, c], yr.at[turn, c, 1], left_y),
+        )
         return [
             pltpu.make_async_remote_copy(
-                src_ref=src.at[turn, out_side],
-                dst_ref=dst.at[turn, in_side],
-                send_sem=rim_send.at[turn, k],
-                recv_sem=rim_recv.at[turn, k],
+                src_ref=src,
+                dst_ref=dst,
+                send_sem=rim_send.at[turn, c, k],
+                recv_sem=rim_recv.at[turn, c, k],
                 device_id=target,
                 device_id_type=MESH,
             )
-            for k, (src, dst, out_side, in_side, target) in enumerate(plan)
+            for k, (src, dst, target) in enumerate(plan)
         ]
 
-    def for_tiles(body):
-        def channel(c, packed):
-            low, high = jnp.zeros((8, 128), F32), jnp.zeros((8, 128), F32)
-            edge = None
-            for z in range(layers):
-                at = pl.ds(pl.multiple_of(c * cell_rows + z * 8, 8), 8)
-                edge = body(c, z, at)
-                if edge is not None:
-                    low = jnp.where(lane == z, pltpu.roll(edge, z, axis=1) if z else edge, low)
-                    high = jnp.where(lane == z, pltpu.roll(edge, z + 1, axis=1), high)
-            if edge is None:
-                return packed
-            ours = (lane >= c * layers) & (lane < (c + 1) * layers)
-            low = jnp.where(ours, pltpu.roll(low, c * layers, axis=1), packed[0])
-            high = jnp.where(ours, pltpu.roll(high, c * layers, axis=1), packed[1])
-            return low, high
-
-        return lax.fori_loop(0, 4, channel, zero_packed)
-
-    def send_rims(turn, field, packed):
-        xs[turn, 0] = field[pl.ds(0, tiles, stride=8), :]
-        xs[turn, 1] = field[pl.ds(7, tiles, stride=8), :]
-        ys[turn, 0] = packed[0]
-        ys[turn, 1] = packed[1]
-        for copy in rim_copies(turn):
+    def tile_of(c, z):
+        return pl.ds(pl.multiple_of(c * cell_rows + z * 8, 8), 8)
+
+    def pack(z, value, packed):
+        return jnp.where((lane >> 1) == z, pltpu.roll(value, 2 * z + 1, axis=1), packed)
+
+    def send_rims(turn, c, field, packed):
+        mine = pl.ds(pl.multiple_of(c * layers, layers), layers)
+        xs[turn, 0, mine, :] = field[pl.ds(c * cell_rows, layers, stride=8), :]
+        xs[turn, 1, mine, :] = field[pl.ds(c * cell_rows + 7, layers, stride=8), :]
+        ys[turn, c] = packed
+        for copy in rim_copies(turn, c):
             copy.start()
 
-    def wait_rims(turn):
-        for copy in rim_copies(turn):
+    def open_rims(turn, c):
+        for copy in rim_copies(turn, c):
             copy.wait()
-
-    def mask_rims(turn):
-        for side, edge_x, edge_y in ((0, 0, 0), (1, n_gx - 1, n_gy - 1)):
-            xr[turn, side] = jnp.where(gx == edge_x, 0.0, xr[turn, side])
-            yr[turn, side] = jnp.where(gy == edge_y, 0.0, yr[turn, side])
-
-    zero_packed = (jnp.zeros((8, 128), F32), jnp.zeros((8, 128), F32))
-
-    def neighbours(turn, field, c, z, at):
-        value = field[at, :]
+        mine = pl.ds(pl.multiple_of(c * layers, layers), layers)
+        xr[turn, 0, mine, :] = jnp.where(gx == 0, 0.0, xr[turn, 0, mine, :])
+        xr[turn, 1, mine, :] = jnp.where(gx == n_gx - 1, 0.0, xr[turn, 1, mine, :])
+        low = jnp.where(gy == 0, 0.0, yr[turn, c, 0])
+        high = jnp.where(gy == n_gy - 1, 0.0, yr[turn, c, 1])
+        return jnp.where((lane & 1) == 0, low, pltpu.roll(high, 126, axis=1))
+
+    def neighbours(turn, field, c, z, columns):
+        value = field[tile_of(c, z), :]
         row = c * layers + z
-        y_low = pltpu.roll(yr[turn, 0], lax.rem(128 - row, 128), axis=1)
-        y_high = pltpu.roll(yr[turn, 1], 127 - row, axis=1)
-        total = jnp.where(sub == 0, jnp.broadcast_to(xr[turn, 0, pl.ds(row, 1), :], (8, 128)), pltpu.roll(value, 1, axis=0))
-        total = total + jnp.where(
-            sub == 7, jnp.broadcast_to(xr[turn, 1, pl.ds(row, 1), :], (8, 128)), pltpu.roll(value, 7, axis=0)
-        )
-        total = total + jnp.where(lane == 0, y_low, pltpu.roll(value, 1, axis=1))
-        total = total + jnp.where(lane == 127, y_high, pltpu.roll(value, 127, axis=1))
+        column = pltpu.roll(columns, 128 - 2 * z, axis=1) if z else columns
+        x_low = jnp.broadcast_to(xr[turn, 0, pl.ds(row, 1), :], (8, 128))
+        x_high = jnp.broadcast_to(xr[turn, 1, pl.ds(row, 1), :], (8, 128))
+        total = jnp.where(sub == 0, x_low, pltpu.roll(value, 1, axis=0))
+        total = total + jnp.where(sub == 7, x_high, pltpu.roll(value, 7, axis=0))
+        total = total + jnp.where(lane == 0, column, pltpu.roll(value, 1, axis=1))
+        total = total + jnp.where(lane == 127, column, pltpu.roll(value, 127, axis=1))
         if z > 0:
-            total = total + field[pl.ds(pl.multiple_of(c * cell_rows + z * 8 - 8, 8), 8), :]
+            total = total + field[tile_of(c, z - 1), :]
         if z < layers - 1:
-            total = total + field[pl.ds(pl.multiple_of(c * cell_rows + z * 8 + 8, 8), 8), :]
+            total = total + field[tile_of(c, z + 1), :]
         return value, total
+
+    no_columns = jnp.zeros((8, 128), F32)
+
+    def split_channel(c):
+        high, low = halves(state_out[pl.ds(pl.multiple_of(c * cell_rows, cell_rows), cell_rows), :])
+        split[c, :, 0:128] = high
+        split[c, :, 128:256] = low
+
+    def split_first(c, carry):
+        split_channel(c)
+        return carry
+
+    lax.fori_loop(0, 4, split_first, 0)
 
     def block_copy(source, target, source_slot, target_slot, device, send_sem, recv_sem):
         return pltpu.make_async_remote_copy(
@@ -185,13 +189,6 @@
 
     def newton(n, carry):
         turn = n * SWEEPS
-
-        send_rims(turn, state_out, for_tiles(lambda c, z, at: state_out[at, :]))
-
-        for c in range(4):
-            high, low = halves(state_out[c * cell_rows : (c + 1) * cell_rows, :])
-            split[c, :, 0:128] = high
-            split[c, :, 128:256] = low
 
         def gather_pair(pair):
             index = jnp.concatenate([cells[pl.ds(2 * pair + k, 1), :] for k in range(2)], axis=1)
@@ -208,34 +205,69 @@
         my_pair = lax.div(me, 2)
         pairs = devices // 2
 
-        def gather_step(step, inner):
-            pair = lax.rem(my_pair + 1 + step, pairs)
-            for k, block in enumerate(gather_pair(pair)):
-                send1[n, 2 * pair + k] = block
-                block_copy(
-                    send1.at[n], recv1.at[n], 2 * pair + k, me, 2 * pair + k, send1_sem.at[n], recv1_sem.at[n]
-                ).start()
-            return inner
-
-        lax.fori_loop(0, pairs - 1, gather_step, 0, unroll=7)
-        for k, block in enumerate(gather_pair(my_pair)):
-            send1[n, 2 * my_pair + k] = block
-        partner = 4 * my_pair + 1 - me
-        block_copy(
-            send1.at[n], recv1.at[n], partner, me, partner, send1_sem.at[n], recv1_sem.at[n]
-        ).start()
+        def pair_of(chunk, k):
+            return lax.rem(my_pair + 1 + chunk * CHUNK + k, pairs)
+
+        def gather_chunk(chunk):
+            for k in range(CHUNK):
+                pair = pair_of(chunk, k)
+                for side, block in enumerate(gather_pair(pair)):
+                    send1[n, 2 * pair + side] = block
+
+        def send_block(target):
+            block_copy(send1.at[n], recv1.at[n], target, me, target, send1_sem.at[n], recv1_sem.at[n]).start()
+
+        def send_chunk(chunk, count=CHUNK):
+            for k in range(count):
+                for side in range(2):
+                    send_block(2 * pair_of(chunk, k) + side)
+
+        chunks = pairs // CHUNK
+        early = chunks // 2
+
+        def early_step(chunk, inner):
+            gather_chunk(chunk)
+            return inner
+
+        lax.fori_loop(0, early, early_step, 0)
+
+        @pl.when(n == 0)
+        def _():
+            pl.semaphore_wait(barrier, devices - 1)
+
+            def first_rims(c, inner):
+                packed = no_columns
+                for z in range(layers):
+                    packed = pack(z, state_out[tile_of(c, z), :], packed)
+                send_rims(turn, c, state_out, packed)
+                return inner
+
+            lax.fori_loop(0, 4, first_rims, 0)
+
+        def late_step(step, inner):
+            send_chunk(2 * step)
+            send_chunk(2 * step + 1)
+            gather_chunk(early + step)
+            return inner
+
+        lax.fori_loop(0, chunks - early - 1, late_step, 0)
+        send_chunk(chunks - 2)
+        gather_chunk(chunks - 1)
+        send_chunk(chunks - 1, CHUNK - 1)
+        send_block(4 * my_pair + 1 - me)
         recv1[n, me] = send1[n, me]
 
-        wait_rims(turn)
-        mask_rims(turn)
-
-        def base(c, z, at):
-            value, near = neighbours(turn, state_out, c, z, at)
-            square = value * value
-            forcing[at, :] = coeff[at, :] * value - near + 0.1 * square * value - right[at, :]
-            factor[at, :] = 1.0 / (coeff[at, :] + 0.3 * square)
-
-        for_tiles(base)
+        def base(c, inner):
+            columns = open_rims(turn, c)
+            for z in range(layers):
+                at = tile_of(c, z)
+                value, near = neighbours(turn, state_out, c, z, columns)
+                square = value * value
+                forcing[at, :] = coeff[at, :] * value - near + 0.1 * square * value - right[at, :]
+                factor[at, :] = 1.0 / (coeff[at, :] + 0.3 * square)
+            return inner
+
+        lax.fori_loop(0, 4, base, 0)
 
         all_blocks = pl.ds(0, devices - 1)
         arrived = pltpu.make_async_remote_copy(
@@ -287,7 +319,10 @@
         rows[1] = rates[:, 128:]
         total3[...] = jnp.zeros_like(total3)
 
-        def owner_scatter(step, inner):
+        def group_start(j):
+            return lax.rem(my_group + j, GROUPS) * group
+
+        def owner_scatter(j, step):
             first_well = step * WELLS_STEP
             width = WELLS_STEP * 256
             index = jnp.concatenate([slots[pl.ds(first_well + k, 1), :] for k in range(WELLS_STEP)], axis=1)
@@ -296,32 +331,46 @@
                 axis=1,
             )
             pick = onehot(128, index & 127)
-            wanted = (lax.broadcasted_iota(jnp.int32, (4 * devices, width), 0) >> 2) == (index >> 7)
+            wanted = (lax.broadcasted_iota(jnp.int32, (4 * group, width), 0) >> 2) == (index >> 7) - group_start(j)
             parts = []
             for half in halves(jnp.concatenate([rate, rate], axis=0)):
-                spread = jnp.broadcast_to(half.astype(F32)[None], (devices // 2, 8, width))
-                parts.append(jnp.where(wanted, spread.reshape(4 * devices, width), 0.0).astype(BF16))
-            total3[...] += lax.dot_general(
+                spread = jnp.broadcast_to(half.astype(F32)[None], (group // 2, 8, width))
+                parts.append(jnp.where(wanted, spread.reshape(4 * group, width), 0.0).astype(BF16))
+            total3[j] += lax.dot_general(
                 jnp.concatenate(parts, axis=1),
                 jnp.concatenate([pick, pick], axis=1),
                 (((1,), (1,)), ((), ())),
                 preferred_element_type=F32,
             )
-            return inner
-
-        lax.fori_loop(0, wells // WELLS_STEP, owner_scatter, 0)
-        send2[n] = total3[...].reshape(devices, 4, 128)
+
+        def return_block(j, step):
+            target = group_start(j) + lax.rem(me + step, group)
+            block_copy(send2.at[n], recv2.at[n], target, me, target, send2_sem.at[n], recv2_sem.at[n, j]).start()
+
+        well_steps = wells // WELLS_STEP
+        each = group // well_steps
+
+        def own_half(step, inner):
+            owner_scatter(0, step)
+            return inner
+
+        lax.fori_loop(0, well_steps, own_half, 0)
+        send2[n, pl.ds(group_start(0), group)] = total3[0].reshape(group, 4, 128)
         recv2[n, me] = send2[n, me]
 
-        def return_step(step, inner):
-            j = lax.div(step, group)
-            target = lax.rem(my_group + j, GROUPS) * group + lax.rem(me + step, group)
-            block_copy(
-                send2.at[n], recv2.at[n], target, me, target, send2_sem.at[n], recv2_sem.at[n, j]
-            ).start()
-            return inner
-
-        lax.fori_loop(1, devices, return_step, 0)
+        def other_half(step, inner):
+            for k in range(each - 1):
+                return_block(0, 1 + step * each + k)
+
+            @pl.when(step < well_steps - 1)
+            def _():
+                return_block(0, each + step * each)
+
+            owner_scatter(1, step)
+            return inner
+
+        lax.fori_loop(0, well_steps, other_half, 0)
+        send2[n, pl.ds(group_start(1), group)] = total3[1].reshape(group, 4, 128)
         arrived.wait_send()
 
         total4[...] = jnp.zeros_like(total4)
@@ -338,9 +387,12 @@
             ).wait_recv()
 
         def inflow_group(j):
-            start = lax.rem(my_group + GROUPS - j, GROUPS) * group
+            start = group_start(j)
 
             def inflow_step(step, inner):
+                if j == 0:
+                    for k in range(STEP):
+                        return_block(1, step * STEP + k)
                 owner = start + step * STEP
                 index = jnp.concatenate([cells[pl.ds(owner + k, 1), :] for k in range(STEP)], axis=1)
                 value = jnp.concatenate([recv2[n, owner + k] for k in range(STEP)], axis=1)
@@ -377,31 +429,48 @@
             device_id_type=MESH,
         ).wait_send()
 
-        for c in range(4):
-            at = slice(c * cell_rows, (c + 1) * cell_rows)
-            forcing[at, :] = forcing[at, :] - total4[:, c * 128 : (c + 1) * 128]
-
-        def first_sweep(c, z, at):
-            value = forcing[at, :] * factor[at, :]
-            corr[0, at, :] = value
-            return value
-
-        packed = for_tiles(first_sweep)
+        def first_sweep(c, inner):
+            packed = no_columns
+            for z in range(layers):
+                at = tile_of(c, z)
+                inflow = total4[z * 8 : z * 8 + 8, pl.ds(pl.multiple_of(c * 128, 128), 128)]
+                value = forcing[at, :] - inflow
+                forcing[at, :] = value
+                value = value * factor[at, :]
+                corr[0, at, :] = value
+                packed = pack(z, value, packed)
+            send_rims(turn + 1, c, corr.at[0], packed)
+            return inner
+
+        lax.fori_loop(0, 4, first_sweep, 0)
         for k in range(1, SWEEPS):
             now, later = corr.at[(k - 1) % 2], corr.at[k % 2]
-            send_rims(turn + k, now, packed)
-            wait_rims(turn + k)
-            mask_rims(turn + k)
-
-            def sweep(c, z, at):
-                _, near = neighbours(turn + k, now, c, z, at)
-                value = (forcing[at, :] + near) * factor[at, :]
+
+            def sweep(c, inner):
+                columns = open_rims(turn + k, c)
+                packed = no_columns
+                for z in range(layers):
+                    at = tile_of(c, z)
+                    _, near = neighbours(turn + k, now, c, z, columns)
+                    value = (forcing[at, :] + near) * factor[at, :]
+                    if k < SWEEPS - 1:
+                        later[at, :] = value
+                    else:
+                        value = state_out[at, :] - value
+                        state_out[at, :] = value
+                    packed = pack(z, value, packed)
                 if k < SWEEPS - 1:
-                    later[at, :] = value
-                    return value
-                state_out[at, :] = state_out[at, :] - value
-
-            packed = for_tiles(sweep)
+                    send_rims(turn + k + 1, c, later, packed)
+                else:
+
+                    @pl.when(n < NEWTON - 1)
+                    def _():
+                        send_rims(turn + SWEEPS, c, state_out, packed)
+                        split_channel(c)
+
+                return inner
+
+            lax.fori_loop(0, 4, sweep, 0)
         return carry
 
     lax.fori_loop(0, NEWTON, newton, 0)
@@ -445,19 +514,19 @@
             pltpu.VMEM((2, channels * wells, 128), F32),
             pltpu.VMEM((NEWTON, devices, channels, 128), F32),
             pltpu.VMEM((NEWTON, devices, channels, 128), F32),
-            pltpu.VMEM((channels * devices, 128), F32),
+            pltpu.VMEM((GROUPS, channels * devices // GROUPS, 128), F32),
             pltpu.VMEM((cell_rows, channels * 128), F32),
             pltpu.VMEM((segments, segments), F32),
             pltpu.VMEM((turns, 2, tiles, 128), F32),
             pltpu.VMEM((turns, 2, tiles, 128), F32),
-            pltpu.VMEM((turns, 2, 8, 128), F32),
-            pltpu.VMEM((turns, 2, 8, 128), F32),
+            pltpu.VMEM((turns, channels, 8, 128), F32),
+            pltpu.VMEM((turns, channels, 2, 8, 128), F32),
             dma((NEWTON,)),
             dma((NEWTON,)),
             dma((NEWTON,)),
             dma((NEWTON, GROUPS)),
-            dma((turns, 4)),
-            dma((turns, 4)),
+            dma((turns, channels, 4)),
+            dma((turns, channels, 4)),
         ],
         compiler_params=pltpu.CompilerParams(
             collective_id=0, has_side_effects=True, vmem_limit_bytes=62 * 1024 * 1024

time: 150 us -> 136 us (0.907)
  Pallas kernels: 146 us -> 132 us
    pallas_call x1, Pallas kernels: 146 us -> 132 us  [on_device(): pl.pallas_call(functools.partial(kernel, n_gx, n_gy, layers, wells), out_...]
where the time goes in v3:
time: 136 us; the launch traced here: 135 us
  Pallas kernels  132 us (97%)
  local copies, waits for them, and re-layouts  2.56 us (2%)
    pallas_call x1, Pallas kernels, on_device(): pl.pallas_call(functools.partial(kernel, n_gx, n_gy, layers, wells), out_...  132 us

profile of v3, /device:TPU:1, one launch (start us, length us, event | category | flops | bytes accessed | tf_op | source)
XLA Modules:
  0.0 134.9 jit_solution(11895860330942991137)
XLA Ops:
  0.6 131.7 %newton.1 = (f32[1024,128]{1,0:T(8,128)}, f32[128,256]{1,0:T(8,128)}) custom-call(f32[1024,128]{1,0:T(8,128)} %bitcast.7, f32[1024,128]{1,0:T(8,128)} %bitcast.8, s32[256,128]{1,0:T(8,128)} %bitcast.10, f32[4,8]{1,0:T(4,128)} %table.1, s32[128,128]{1,0:T(8,128)} %bitcast.11, s32[32,256]{1,0:T(8,128)} %slots_in.1, f32[4,4,32,256]{3,2,1,0:T(8,128)} %inverse_in.1), custom_call_target="tpu_custom_call" | custom-call | tf_op jit(solution)/shard_map/newton/pallas_call | solution.py:491
  132.3 0.0 copy-start
  132.3 1.9 %copy.11 = f32[4,32,8,128]{3,2,1,0:T(8,128)} copy(f32[4,32,8,128]{3,2,1,0:T(8,128)} %bitcast.6) | data formatting | bytes 1048576
  134.2 0.0 copy-done
  134.2 0.7 copy.12
Async XLA Ops:
  132.3 1.9 %copy-start = (f32[128,256]{1,0:T(8,128)S(1)}, f32[128,256]{1,0:T(8,128)}, u32[]{:S(2)}) copy-start(f32[128,256]{1,0:T(8,128)} %get-tuple-element.5) | copy-start | bytes 393220

commit v4 on v3

--- a/solution.py
+++ b/solution.py
@@ -9,8 +9,9 @@
 
 NEWTON = 2
 SWEEPS = 4
-GROUPS = 2
-STEP = 16
+PLANES = 4
+PLANE_ORDER = (0, 1, 3, 2)
+CHUNK_ORDER = (10, 9, 11, 6, 14, 5, 7, 13, 15, 8, 2, 4, 12, 1, 3, 0)
 WELLS_STEP = 8
 CHUNK = 4
 F32 = jnp.float32
@@ -42,7 +43,7 @@
     me = gx * n_gy + gy
     cell_rows = layers * 8
     tiles = 4 * layers
-    group = devices // GROUPS
+    group = devices // PLANES
     my_group = lax.div(me, group)
 
     def place(device):
@@ -202,11 +203,19 @@
             found = jnp.concatenate(found, axis=0)
             return found[:, :128], found[:, 128:]
 
+
         my_pair = lax.div(me, 2)
         pairs = devices // 2
 
         def pair_of(chunk, k):
-            return lax.rem(my_pair + 1 + chunk * CHUNK + k, pairs)
+            away = 0
+            for i, code in enumerate(CHUNK_ORDER):
+                away = jnp.where(chunk == i, code, away)
+            chip_x = lax.rem(lax.div(gx, 2) + lax.div(away, 4), 4)
+            core = lax.rem(gx + 1 - k // 2, 2)
+            chip_z = lax.rem(lax.div(gy, 4) + lax.rem(away, 4), 4)
+            half_y = lax.rem(lax.div(gy, 2) + 1 - k % 2, 2)
+            return (2 * chip_x + core) * (n_gy // 2) + chip_z * 2 + half_y
 
         def gather_chunk(chunk):
             for k in range(CHUNK):
@@ -319,10 +328,10 @@
         rows[1] = rates[:, 128:]
         total3[...] = jnp.zeros_like(total3)
 
-        def group_start(j):
-            return lax.rem(my_group + j, GROUPS) * group
-
-        def owner_scatter(j, step):
+        def plane_start(away):
+            return lax.rem(my_group + away, PLANES) * group
+
+        def owner_scatter(side, step):
             first_well = step * WELLS_STEP
             width = WELLS_STEP * 256
             index = jnp.concatenate([slots[pl.ds(first_well + k, 1), :] for k in range(WELLS_STEP)], axis=1)
@@ -331,49 +340,45 @@
                 axis=1,
             )
             pick = onehot(128, index & 127)
-            wanted = (lax.broadcasted_iota(jnp.int32, (4 * group, width), 0) >> 2) == (index >> 7) - group_start(j)
+            row = lax.broadcasted_iota(jnp.int32, (8 * group, width), 0)
+            near, far = (plane_start(PLANE_ORDER[2 * side + k]) for k in range(2))
+            device = jnp.where(row < 4 * group, near, far - group) + (row >> 2)
+            wanted = device == (index >> 7)
             parts = []
             for half in halves(jnp.concatenate([rate, rate], axis=0)):
-                spread = jnp.broadcast_to(half.astype(F32)[None], (group // 2, 8, width))
-                parts.append(jnp.where(wanted, spread.reshape(4 * group, width), 0.0).astype(BF16))
-            total3[j] += lax.dot_general(
+                spread = jnp.broadcast_to(half.astype(F32)[None], (group, 8, width))
+                parts.append(jnp.where(wanted, spread.reshape(8 * group, width), 0.0).astype(BF16))
+            total3[side] += lax.dot_general(
                 jnp.concatenate(parts, axis=1),
                 jnp.concatenate([pick, pick], axis=1),
                 (((1,), (1,)), ((), ())),
                 preferred_element_type=F32,
             )
 
-        def return_block(j, step):
-            target = group_start(j) + lax.rem(me + step, group)
-            block_copy(send2.at[n], recv2.at[n], target, me, target, send2_sem.at[n], recv2_sem.at[n, j]).start()
-
-        well_steps = wells // WELLS_STEP
-        each = group // well_steps
-
-        def own_half(step, inner):
-            owner_scatter(0, step)
-            return inner
-
-        lax.fori_loop(0, well_steps, own_half, 0)
-        send2[n, pl.ds(group_start(0), group)] = total3[0].reshape(group, 4, 128)
-        recv2[n, me] = send2[n, me]
-
-        def other_half(step, inner):
-            for k in range(each - 1):
-                return_block(0, 1 + step * each + k)
-
-            @pl.when(step < well_steps - 1)
-            def _():
-                return_block(0, each + step * each)
-
-            owner_scatter(1, step)
-            return inner
-
-        lax.fori_loop(0, well_steps, other_half, 0)
-        send2[n, pl.ds(group_start(1), group)] = total3[1].reshape(group, 4, 128)
+        for side in range(2):
+
+            def owner_step(step, inner):
+                owner_scatter(side, step)
+                return inner
+
+            lax.fori_loop(0, wells // WELLS_STEP, owner_step, 0)
+            for k in range(2):
+                j = 2 * side + k
+                start = plane_start(PLANE_ORDER[j])
+                send2[n, pl.ds(start, group)] = total3[side, 4 * group * k : 4 * group * (k + 1)].reshape(group, 4, 128)
+
+                def return_step(step, inner):
+                    target = start + lax.rem(me + step, group)
+                    block_copy(
+                        send2.at[n], recv2.at[n], target, me, target, send2_sem.at[n], recv2_sem.at[n, j]
+                    ).start()
+                    return inner
+
+                lax.fori_loop(1 if j == 0 else 0, group, return_step, 0)
+            if side == 0:
+                recv2[n, me] = send2[n, me]
         arrived.wait_send()
 
-        total4[...] = jnp.zeros_like(total4)
 
         def wait_group(j, count):
             some = pl.ds(0, count)
@@ -386,39 +391,27 @@
                 device_id_type=MESH,
             ).wait_recv()
 
-        def inflow_group(j):
-            start = group_start(j)
-
-            def inflow_step(step, inner):
-                if j == 0:
-                    for k in range(STEP):
-                        return_block(1, step * STEP + k)
-                owner = start + step * STEP
-                index = jnp.concatenate([cells[pl.ds(owner + k, 1), :] for k in range(STEP)], axis=1)
-                value = jnp.concatenate([recv2[n, owner + k] for k in range(STEP)], axis=1)
-                lanes = onehot(128, index & 127)
-                pick = onehot(cell_rows, index >> 7)
-                pick = jnp.concatenate([pick, pick], axis=1)
-                high, low = halves(value)
-                spread = jnp.concatenate(
-                    [
-                        jnp.concatenate([lanes * high[c : c + 1], lanes * low[c : c + 1]], axis=1)
-                        for c in range(4)
-                    ],
-                    axis=0,
-                )
-                total4[...] += lax.dot_general(
-                    pick, spread, (((1,), (1,)), ((), ())), preferred_element_type=F32
-                )
-                return inner
-
-            lax.fori_loop(0, group // STEP, inflow_step, 0)
-
-        wait_group(0, group - 1)
-        inflow_group(0)
-        for j in range(1, GROUPS):
-            wait_group(j, group)
-            inflow_group(j)
+        for j in range(PLANES):
+            wait_group(j, group - 1 if j == 0 else group)
+            start = lax.rem(my_group + PLANES - PLANE_ORDER[j], PLANES) * group
+            index = jnp.concatenate([cells[pl.ds(start + k, 1), :] for k in range(group)], axis=1)
+            value = jnp.concatenate([recv2[n, start + k] for k in range(group)], axis=1)
+            lanes = onehot(128, index & 127)
+            pick = onehot(cell_rows, index >> 7)
+            pick = jnp.concatenate([pick, pick], axis=1)
+            high, low = halves(value)
+            spread = jnp.concatenate(
+                [
+                    jnp.concatenate([lanes * high[c : c + 1], lanes * low[c : c + 1]], axis=1)
+                    for c in range(4)
+                ],
+                axis=0,
+            )
+            found = lax.dot_general(pick, spread, (((1,), (1,)), ((), ())), preferred_element_type=F32)
+            if j == 0:
+                total4[...] = found
+            else:
+                total4[...] += found
         sent = pl.ds(0, devices - 1)
         pltpu.make_async_remote_copy(
             src_ref=send2.at[n, sent],
@@ -514,7 +507,7 @@
             pltpu.VMEM((2, channels * wells, 128), F32),
             pltpu.VMEM((NEWTON, devices, channels, 128), F32),
             pltpu.VMEM((NEWTON, devices, channels, 128), F32),
-            pltpu.VMEM((GROUPS, channels * devices // GROUPS, 128), F32),
+            pltpu.VMEM((2, channels * devices // 2, 128), F32),
             pltpu.VMEM((cell_rows, channels * 128), F32),
             pltpu.VMEM((segments, segments), F32),
             pltpu.VMEM((turns, 2, tiles, 128), F32),
@@ -524,7 +517,7 @@
             dma((NEWTON,)),
             dma((NEWTON,)),
             dma((NEWTON,)),
-            dma((NEWTON, GROUPS)),
+            dma((NEWTON, PLANES)),
             dma((turns, channels, 4)),
             dma((turns, channels, 4)),
         ],

time: 136 us -> 120 us (0.88)
  Pallas kernels: 132 us -> 117 us
    pallas_call x1, Pallas kernels: 132 us -> 117 us  [on_device(): pl.pallas_call(functools.partial(kernel, n_gx, n_gy, layers, wells), out_...]
where the time goes in v4:
time: 120 us
  Pallas kernels  117 us (98%)
  local copies, waits for them, and re-layouts  2.56 us (2%)
    pallas_call x1, Pallas kernels, on_device(): pl.pallas_call(functools.partial(kernel, n_gx, n_gy, layers, wells), out_...  117 us
    unnamed x4, local copies, waits for them, and re-layouts  2.56 us

profile of v4, /device:TPU:1, one launch (start us, length us, event | category | flops | bytes accessed | tf_op | source)
XLA Modules:
  0.0 119.8 jit_solution(14602774247981834168)
XLA Ops:
  0.6 116.6 %newton.1 = (f32[1024,128]{1,0:T(8,128)}, f32[128,256]{1,0:T(8,128)}) custom-call(f32[1024,128]{1,0:T(8,128)} %bitcast.7, f32[1024,128]{1,0:T(8,128)} %bitcast.8, s32[256,128]{1,0:T(8,128)} %bitcast.10, f32[4,8]{1,0:T(4,128)} %table.1, s32[128,128]{1,0:T(8,128)} %bitcast.11, s32[32,256]{1,0:T(8,128)} %slots_in.1, f32[4,4,32,256]{3,2,1,0:T(8,128)} %inverse_in.1), custom_call_target="tpu_custom_call" | custom-call | tf_op jit(solution)/shard_map/newton/pallas_call | solution.py:484
  117.3 0.0 copy-start
  117.3 1.9 %copy.11 = f32[4,32,8,128]{3,2,1,0:T(8,128)} copy(f32[4,32,8,128]{3,2,1,0:T(8,128)} %bitcast.6) | data formatting | bytes 1048576
  119.2 0.0 copy-done
  119.2 0.7 copy.12
Async XLA Ops:
  117.3 1.9 %copy-start = (f32[128,256]{1,0:T(8,128)S(1)}, f32[128,256]{1,0:T(8,128)}, u32[]{:S(2)}) copy-start(f32[128,256]{1,0:T(8,128)} %get-tuple-element.5) | copy-start | bytes 393220

commit v5 on v4

--- a/solution.py
+++ b/solution.py
@@ -12,7 +12,7 @@
 PLANES = 4
 PLANE_ORDER = (0, 1, 3, 2)
 CHUNK_ORDER = (10, 9, 11, 6, 14, 5, 7, 13, 15, 8, 2, 4, 12, 1, 3, 0)
-WELLS_STEP = 8
+WELLS_STEP = 16
 CHUNK = 4
 F32 = jnp.float32
 BF16 = jnp.bfloat16
@@ -64,6 +64,9 @@
     ]
     for load in loads:
         load.start()
+
+    xr[...] = jnp.zeros_like(xr)
+    yr[...] = jnp.zeros_like(yr)
 
     barrier = pltpu.get_barrier_semaphore()
 
@@ -133,21 +136,38 @@
 
     def send_rims(turn, c, field, packed):
         mine = pl.ds(pl.multiple_of(c * layers, layers), layers)
+        x_up, x_down, y_up, y_down = rim_copies(turn, c)
+        ys[turn, c] = packed
+        start_pair(y_up, y_down, gy, n_gy)
         xs[turn, 0, mine, :] = field[pl.ds(c * cell_rows, layers, stride=8), :]
         xs[turn, 1, mine, :] = field[pl.ds(c * cell_rows + 7, layers, stride=8), :]
-        ys[turn, c] = packed
-        for copy in rim_copies(turn, c):
-            copy.start()
+        start_pair(x_up, x_down, gx, n_gx)
+
+    def start_pair(up, down, position, count):
+        @pl.when(position < count - 1)
+        def _():
+            up.start()
+
+        @pl.when(position > 0)
+        def _():
+            down.start()
+
+    def wait_pair(up, down, position, count):
+        @pl.when(position < count - 1)
+        def _():
+            up.wait_send()
+            down.wait_recv()
+
+        @pl.when(position > 0)
+        def _():
+            down.wait_send()
+            up.wait_recv()
 
     def open_rims(turn, c):
-        for copy in rim_copies(turn, c):
-            copy.wait()
-        mine = pl.ds(pl.multiple_of(c * layers, layers), layers)
-        xr[turn, 0, mine, :] = jnp.where(gx == 0, 0.0, xr[turn, 0, mine, :])
-        xr[turn, 1, mine, :] = jnp.where(gx == n_gx - 1, 0.0, xr[turn, 1, mine, :])
-        low = jnp.where(gy == 0, 0.0, yr[turn, c, 0])
-        high = jnp.where(gy == n_gy - 1, 0.0, yr[turn, c, 1])
-        return jnp.where((lane & 1) == 0, low, pltpu.roll(high, 126, axis=1))
+        x_up, x_down, y_up, y_down = rim_copies(turn, c)
+        wait_pair(x_up, x_down, gx, n_gx)
+        wait_pair(y_up, y_down, gy, n_gy)
+        return jnp.where((lane & 1) == 0, yr[turn, c, 0], pltpu.roll(yr[turn, c, 1], 126, axis=1))
 
     def neighbours(turn, field, c, z, columns):
         value = field[tile_of(c, z), :]
@@ -326,12 +346,11 @@
         rates_out[...] = rates
         rows[0] = rates[:, :128]
         rows[1] = rates[:, 128:]
-        total3[...] = jnp.zeros_like(total3)
 
         def plane_start(away):
             return lax.rem(my_group + away, PLANES) * group
 
-        def owner_scatter(side, step):
+        def owner_scatter(step):
             first_well = step * WELLS_STEP
             width = WELLS_STEP * 256
             index = jnp.concatenate([slots[pl.ds(first_well + k, 1), :] for k in range(WELLS_STEP)], axis=1)
@@ -339,44 +358,40 @@
                 [rows[half, pl.ds(first_well + k, 4, stride=wells), :] for k in range(WELLS_STEP) for half in range(2)],
                 axis=1,
             )
-            pick = onehot(128, index & 127)
-            row = lax.broadcasted_iota(jnp.int32, (8 * group, width), 0)
-            near, far = (plane_start(PLANE_ORDER[2 * side + k]) for k in range(2))
-            device = jnp.where(row < 4 * group, near, far - group) + (row >> 2)
-            wanted = device == (index >> 7)
+            pick = onehot(256, index & 255)
+            wanted = (lax.broadcasted_iota(jnp.int32, (2 * devices, width), 0) >> 2) == (index >> 8)
             parts = []
             for half in halves(jnp.concatenate([rate, rate], axis=0)):
-                spread = jnp.broadcast_to(half.astype(F32)[None], (group, 8, width))
-                parts.append(jnp.where(wanted, spread.reshape(8 * group, width), 0.0).astype(BF16))
-            total3[side] += lax.dot_general(
+                spread = jnp.broadcast_to(half.astype(F32)[None], (devices // 4, 8, width))
+                parts.append(jnp.where(wanted, spread.reshape(2 * devices, width), 0.0).astype(BF16))
+            return lax.dot_general(
                 jnp.concatenate(parts, axis=1),
                 jnp.concatenate([pick, pick], axis=1),
                 (((1,), (1,)), ((), ())),
                 preferred_element_type=F32,
             )
 
-        for side in range(2):
-
-            def owner_step(step, inner):
-                owner_scatter(side, step)
+        total3[...] = owner_scatter(0)
+        for step in range(1, wells // WELLS_STEP):
+            total3[...] += owner_scatter(step)
+        for k in range(2):
+            send2[n, pairs * k : pairs * (k + 1)] = total3[:, 128 * k : 128 * (k + 1)].reshape(pairs, 4, 128)
+
+        def send_slot(device):
+            return lax.rem(device, 2) * pairs + lax.div(device, 2)
+
+        for j in range(PLANES):
+            start = plane_start(PLANE_ORDER[j])
+
+            def return_step(step, inner):
+                target = start + lax.rem(me + step, group)
+                block_copy(
+                    send2.at[n], recv2.at[n], send_slot(target), me, target, send2_sem.at[n], recv2_sem.at[n, j]
+                ).start()
                 return inner
 
-            lax.fori_loop(0, wells // WELLS_STEP, owner_step, 0)
-            for k in range(2):
-                j = 2 * side + k
-                start = plane_start(PLANE_ORDER[j])
-                send2[n, pl.ds(start, group)] = total3[side, 4 * group * k : 4 * group * (k + 1)].reshape(group, 4, 128)
-
-                def return_step(step, inner):
-                    target = start + lax.rem(me + step, group)
-                    block_copy(
-                        send2.at[n], recv2.at[n], target, me, target, send2_sem.at[n], recv2_sem.at[n, j]
-                    ).start()
-                    return inner
-
-                lax.fori_loop(1 if j == 0 else 0, group, return_step, 0)
-            if side == 0:
-                recv2[n, me] = send2[n, me]
+            lax.fori_loop(1 if j == 0 else 0, group, return_step, 0)
+        recv2[n, me] = send2[n, send_slot(me)]
         arrived.wait_send()
 
 
@@ -507,7 +522,7 @@
             pltpu.VMEM((2, channels * wells, 128), F32),
             pltpu.VMEM((NEWTON, devices, channels, 128), F32),
             pltpu.VMEM((NEWTON, devices, channels, 128), F32),
-            pltpu.VMEM((2, channels * devices // 2, 128), F32),
+            pltpu.VMEM((channels * devices // 2, 256), F32),
             pltpu.VMEM((cell_rows, channels * 128), F32),
             pltpu.VMEM((segments, segments), F32),
             pltpu.VMEM((turns, 2, tiles, 128), F32),

time: 120 us -> 131 us (1.092)
  Pallas kernels: 117 us -> 126 us
    pallas_call x1, Pallas kernels: 117 us -> 126 us  [on_device(): pl.pallas_call(functools.partial(kernel, n_gx, n_gy, layers, wells), out_...]
where the time goes in v5:
time: 131 us; the launch traced here: 130 us
  Pallas kernels  126 us (96%)
  local copies, waits for them, and re-layouts  2.56 us (2%)
    pallas_call x1, Pallas kernels, on_device(): pl.pallas_call(functools.partial(kernel, n_gx, n_gy, layers, wells), out_...  126 us

profile of v5, /device:TPU:1, one launch (start us, length us, event | category | flops | bytes accessed | tf_op | source)
XLA Modules:
  0.0 129.7 jit_solution(4882021840829124678)
XLA Ops:
  0.6 126.4 %newton.1 = (f32[1024,128]{1,0:T(8,128)}, f32[128,256]{1,0:T(8,128)}) custom-call(f32[1024,128]{1,0:T(8,128)} %bitcast.7, f32[1024,128]{1,0:T(8,128)} %bitcast.8, s32[256,128]{1,0:T(8,128)} %bitcast.10, f32[4,8]{1,0:T(4,128)} %table.1, s32[128,128]{1,0:T(8,128)} %bitcast.11, s32[32,256]{1,0:T(8,128)} %slots_in.1, f32[4,4,32,256]{3,2,1,0:T(8,128)} %inverse_in.1), custom_call_target="tpu_custom_call" | custom-call | tf_op jit(solution)/shard_map/newton/pallas_call | solution.py:499
  127.1 0.0 copy-start
  127.1 1.9 %copy.11 = f32[4,32,8,128]{3,2,1,0:T(8,128)} copy(f32[4,32,8,128]{3,2,1,0:T(8,128)} %bitcast.6) | data formatting | bytes 1048576
  129.0 0.0 copy-done
  129.0 0.7 copy.12
Async XLA Ops:
  127.1 1.9 %copy-start = (f32[128,256]{1,0:T(8,128)S(1)}, f32[128,256]{1,0:T(8,128)}, u32[]{:S(2)}) copy-start(f32[128,256]{1,0:T(8,128)} %get-tuple-element.5) | copy-start | bytes 393220

commit v6 on v5

--- a/solution.py
+++ b/solution.py
@@ -34,7 +34,7 @@
     state_in, right_in, rock_in, table, cells_in, slots_in, inverse_in,
     state_out, rates_out,
     right, rock, cells, slots, inverse, load_sem,
-    coeff, forcing, factor, corr, split, send1, recv1, split2, rows, send2, recv2, total3, total4, decay,
+    coeff, forcing, factor, corr, split, send1, recv1, split2, rows, send2, recv2, total3, total4, decay, lane_hot, row_hot,
     xs, xr, ys, yr,
     send1_sem, recv1_sem, send2_sem, recv2_sem, rim_send, rim_recv,
 ):
@@ -53,9 +53,9 @@
         pltpu.make_async_copy(source, target, load_sem.at[k])
         for k, (source, target) in enumerate(
             (
-                (rock_in, rock),
                 (state_in, state_out),
                 (cells_in, cells),
+                (rock_in, rock),
                 (right_in, right),
                 (slots_in, slots),
                 (inverse_in, inverse),
@@ -78,27 +78,7 @@
 
     lax.fori_loop(1, devices, greet, 0)
 
-    loads[0].wait()
-
-    def coefficients(i, inner):
-        at = pl.ds(pl.multiple_of(i * 8, 8), 8)
-        kinds = rock[at, :]
-        picked = [kinds == kind for kind in range(8)]
-        for c in range(4):
-            value = jnp.full((8, 128), 6.0, F32)
-            for kind in range(8):
-                value = value + jnp.where(picked[kind], table[c, kind], 0.0)
-            coeff[pl.ds(pl.multiple_of(c * cell_rows + i * 8, 8), 8), :] = value
-        return inner
-
-    lax.fori_loop(0, layers, coefficients, 0, unroll=2)
-    first = lax.broadcasted_iota(jnp.int32, decay.shape, 0)
-    second = lax.broadcasted_iota(jnp.int32, decay.shape, 1)
-    gap = (second - first).astype(F32)
-    decay[...] = jnp.where(
-        gap >= 0, 0.3 * jnp.exp(jnp.maximum(gap, 0.0) * -0.10536051565782628), 0.0
-    )
-    for load in loads[1:]:
+    for load in loads[:2]:
         load.wait()
 
     lane = lax.broadcasted_iota(jnp.int32, (8, 128), 1)
@@ -254,37 +234,59 @@
         chunks = pairs // CHUNK
         early = chunks // 2
 
-        def early_step(chunk, inner):
+        def gather_step(chunk, inner):
+            @pl.when((chunk == early) & (n == 0))
+            def _():
+                pl.semaphore_wait(barrier, devices - 1)
+
+                def first_rims(c, rest):
+                    packed = no_columns
+                    for z in range(layers):
+                        packed = pack(z, state_out[tile_of(c, z), :], packed)
+                    send_rims(turn, c, state_out, packed)
+                    return rest
+
+                lax.fori_loop(0, 4, first_rims, 0)
+
+            @pl.when(chunk >= early)
+            def _():
+                send_chunk(2 * (chunk - early))
+
+            @pl.when((chunk >= early) & (chunk < chunks - 1))
+            def _():
+                send_chunk(2 * (chunk - early) + 1)
+
             gather_chunk(chunk)
             return inner
 
-        lax.fori_loop(0, early, early_step, 0)
-
-        @pl.when(n == 0)
-        def _():
-            pl.semaphore_wait(barrier, devices - 1)
-
-            def first_rims(c, inner):
-                packed = no_columns
-                for z in range(layers):
-                    packed = pack(z, state_out[tile_of(c, z), :], packed)
-                send_rims(turn, c, state_out, packed)
-                return inner
-
-            lax.fori_loop(0, 4, first_rims, 0)
-
-        def late_step(step, inner):
-            send_chunk(2 * step)
-            send_chunk(2 * step + 1)
-            gather_chunk(early + step)
-            return inner
-
-        lax.fori_loop(0, chunks - early - 1, late_step, 0)
-        send_chunk(chunks - 2)
-        gather_chunk(chunks - 1)
+        lax.fori_loop(0, chunks, gather_step, 0)
         send_chunk(chunks - 1, CHUNK - 1)
         send_block(4 * my_pair + 1 - me)
         recv1[n, me] = send1[n, me]
+
+        @pl.when(n == 0)
+        def _():
+            for load in loads[2:]:
+                load.wait()
+
+            def coefficients(i, inner):
+                at = pl.ds(pl.multiple_of(i * 8, 8), 8)
+                kinds = rock[at, :]
+                picked = [kinds == kind for kind in range(8)]
+                for c in range(4):
+                    value = jnp.full((8, 128), 6.0, F32)
+                    for kind in range(8):
+                        value = value + jnp.where(picked[kind], table[c, kind], 0.0)
+                    coeff[pl.ds(pl.multiple_of(c * cell_rows + i * 8, 8), 8), :] = value
+                return inner
+
+            lax.fori_loop(0, layers, coefficients, 0, unroll=2)
+            first = lax.broadcasted_iota(jnp.int32, decay.shape, 0)
+            second = lax.broadcasted_iota(jnp.int32, decay.shape, 1)
+            gap = (second - first).astype(F32)
+            decay[...] = jnp.where(
+                gap >= 0, 0.3 * jnp.exp(jnp.maximum(gap, 0.0) * -0.10536051565782628), 0.0
+            )
 
         def base(c, inner):
             columns = open_rims(turn, c)
@@ -371,17 +373,26 @@
                 preferred_element_type=F32,
             )
 
-        total3[...] = owner_scatter(0)
-        for step in range(1, wells // WELLS_STEP):
+        def owner_step(step, inner):
             total3[...] += owner_scatter(step)
+            return inner
+
+        total3[...] = jnp.zeros_like(total3)
+        lax.fori_loop(0, wells // WELLS_STEP, owner_step, 0)
         for k in range(2):
             send2[n, pairs * k : pairs * (k + 1)] = total3[:, 128 * k : 128 * (k + 1)].reshape(pairs, 4, 128)
 
         def send_slot(device):
             return lax.rem(device, 2) * pairs + lax.div(device, 2)
 
-        for j in range(PLANES):
-            start = plane_start(PLANE_ORDER[j])
+        def plane_away(j):
+            away = 0
+            for i, plane in enumerate(PLANE_ORDER):
+                away = jnp.where(j == i, plane, away)
+            return away
+
+        def return_plane(j, carry):
+            start = plane_start(plane_away(j))
 
             def return_step(step, inner):
                 target = start + lax.rem(me + step, group)
@@ -390,7 +401,14 @@
                 ).start()
                 return inner
 
-            lax.fori_loop(1 if j == 0 else 0, group, return_step, 0)
+            @pl.when(j > 0)
+            def _():
+                return_step(0, 0)
+
+            lax.fori_loop(1, group, return_step, 0, unroll=True)
+            return carry
+
+        lax.fori_loop(0, PLANES, return_plane, 0)
         recv2[n, me] = send2[n, send_slot(me)]
         arrived.wait_send()
 
@@ -406,13 +424,33 @@
                 device_id_type=MESH,
             ).wait_recv()
 
-        for j in range(PLANES):
-            wait_group(j, group - 1 if j == 0 else group)
-            start = lax.rem(my_group + PLANES - PLANE_ORDER[j], PLANES) * group
+        def owners_of(j):
+            return lax.rem(my_group + PLANES - plane_away(j), PLANES) * group
+
+        def cells_of(j, inner):
+            start = owners_of(j)
             index = jnp.concatenate([cells[pl.ds(start + k, 1), :] for k in range(group)], axis=1)
+            lane_hot[j] = onehot(128, index & 127)
+            row_hot[j] = onehot(cell_rows, index >> 7)
+            return inner
+
+        @pl.when(n == 0)
+        def _():
+            lax.fori_loop(0, PLANES, cells_of, 0)
+
+        def inflow_plane(j, inner):
+            @pl.when(j == 0)
+            def _():
+                wait_group(j, group - 1)
+
+            @pl.when(j > 0)
+            def _():
+                wait_group(j, group)
+
+            start = owners_of(j)
             value = jnp.concatenate([recv2[n, start + k] for k in range(group)], axis=1)
-            lanes = onehot(128, index & 127)
-            pick = onehot(cell_rows, index >> 7)
+            lanes = lane_hot[j]
+            pick = row_hot[j]
             pick = jnp.concatenate([pick, pick], axis=1)
             high, low = halves(value)
             spread = jnp.concatenate(
@@ -422,11 +460,11 @@
                 ],
                 axis=0,
             )
-            found = lax.dot_general(pick, spread, (((1,), (1,)), ((), ())), preferred_element_type=F32)
-            if j == 0:
-                total4[...] = found
-            else:
-                total4[...] += found
+            total4[...] += lax.dot_general(pick, spread, (((1,), (1,)), ((), ())), preferred_element_type=F32)
+            return inner
+
+        total4[...] = jnp.zeros_like(total4)
+        lax.fori_loop(0, PLANES, inflow_plane, 0)
         sent = pl.ds(0, devices - 1)
         pltpu.make_async_remote_copy(
             src_ref=send2.at[n, sent],
@@ -525,6 +563,8 @@
             pltpu.VMEM((channels * devices // 2, 256), F32),
             pltpu.VMEM((cell_rows, channels * 128), F32),
             pltpu.VMEM((segments, segments), F32),
+            pltpu.VMEM((PLANES, 128, devices // PLANES * 128), BF16),
+            pltpu.VMEM((PLANES, cell_rows, devices // PLANES * 128), BF16),
             pltpu.VMEM((turns, 2, tiles, 128), F32),
             pltpu.VMEM((turns, 2, tiles, 128), F32),
             pltpu.VMEM((turns, channels, 8, 128), F32),

time: 131 us -> 116 us (0.89)
  Pallas kernels: 126 us -> 111 us
    pallas_call x1, Pallas kernels: 126 us -> 111 us  [on_device(): pl.pallas_call(functools.partial(kernel, n_gx, n_gy, layers, wells), out_...]
where the time goes in v6:
time: 116 us; the launch traced here: 114 us
  Pallas kernels  111 us (96%)
  local copies, waits for them, and re-layouts  2.56 us (2%)
    pallas_call x1, Pallas kernels, on_device(): pl.pallas_call(functools.partial(kernel, n_gx, n_gy, layers, wells), out_...  111 us
    unnamed x4, local copies, waits for them, and re-layouts  2.56 us

profile of v6, /device:TPU:1, one launch (start us, length us, event | category | flops | bytes accessed | tf_op | source)
XLA Modules:
  0.0 114.2 jit_solution(1278922713504332308)
XLA Ops:
  0.6 111.0 %newton.1 = (f32[1024,128]{1,0:T(8,128)}, f32[128,256]{1,0:T(8,128)}) custom-call(f32[1024,128]{1,0:T(8,128)} %bitcast.7, f32[1024,128]{1,0:T(8,128)} %bitcast.8, s32[256,128]{1,0:T(8,128)} %bitcast.10, f32[4,8]{1,0:T(4,128)} %table.1, s32[128,128]{1,0:T(8,128)} %bitcast.11, s32[32,256]{1,0:T(8,128)} %slots_in.1, f32[4,4,32,256]{3,2,1,0:T(8,128)} %inverse_in.1), custom_call_target="tpu_custom_call" | custom-call | tf_op jit(solution)/shard_map/newton/pallas_call | solution.py:537
  111.6 0.0 copy-start
  111.6 1.9 %copy.11 = f32[4,32,8,128]{3,2,1,0:T(8,128)} copy(f32[4,32,8,128]{3,2,1,0:T(8,128)} %bitcast.6) | data formatting | bytes 1048576
  113.5 0.0 copy-done
  113.6 0.7 copy.12
Async XLA Ops:
  111.6 1.9 %copy-start = (f32[128,256]{1,0:T(8,128)S(1)}, f32[128,256]{1,0:T(8,128)}, u32[]{:S(2)}) copy-start(f32[128,256]{1,0:T(8,128)} %get-tuple-element.5) | copy-start | bytes 393220

commit v7 on v6

--- a/solution.py
+++ b/solution.py
@@ -234,32 +234,34 @@
         chunks = pairs // CHUNK
         early = chunks // 2
 
-        def gather_step(chunk, inner):
-            @pl.when((chunk == early) & (n == 0))
-            def _():
-                pl.semaphore_wait(barrier, devices - 1)
-
-                def first_rims(c, rest):
-                    packed = no_columns
-                    for z in range(layers):
-                        packed = pack(z, state_out[tile_of(c, z), :], packed)
-                    send_rims(turn, c, state_out, packed)
-                    return rest
-
-                lax.fori_loop(0, 4, first_rims, 0)
-
-            @pl.when(chunk >= early)
-            def _():
-                send_chunk(2 * (chunk - early))
-
-            @pl.when((chunk >= early) & (chunk < chunks - 1))
-            def _():
-                send_chunk(2 * (chunk - early) + 1)
-
+        def early_step(chunk, inner):
             gather_chunk(chunk)
             return inner
 
-        lax.fori_loop(0, chunks, gather_step, 0)
+        lax.fori_loop(0, early, early_step, 0)
+
+        @pl.when(n == 0)
+        def _():
+            pl.semaphore_wait(barrier, devices - 1)
+
+            def first_rims(c, rest):
+                packed = no_columns
+                for z in range(layers):
+                    packed = pack(z, state_out[tile_of(c, z), :], packed)
+                send_rims(turn, c, state_out, packed)
+                return rest
+
+            lax.fori_loop(0, 4, first_rims, 0)
+
+        def late_step(step, inner):
+            send_chunk(2 * step)
+            gather_chunk(early + step)
+            send_chunk(2 * step + 1)
+            return inner
+
+        lax.fori_loop(0, chunks - early - 1, late_step, 0)
+        send_chunk(chunks - 2)
+        gather_chunk(chunks - 1)
         send_chunk(chunks - 1, CHUNK - 1)
         send_block(4 * my_pair + 1 - me)
         recv1[n, me] = send1[n, me]
@@ -328,7 +330,7 @@
             rows[1, pl.ds(w, 4, stride=wells), :] = value[:, 128:]
             return inner
 
-        lax.fori_loop(0, wells, owner_gather, 0, unroll=4)
+        lax.fori_loop(0, wells, owner_gather, 0, unroll=8)
         flows = []
         for i in range(4):
             sides = []

time: 116 us -> 114 us (0.983)
  Pallas kernels: 111 us -> 108 us
    pallas_call x1, Pallas kernels: 111 us -> 108 us  [on_device(): pl.pallas_call(functools.partial(kernel, n_gx, n_gy, layers, wells), out_...]
where the time goes in v7:
time: 114 us; the launch traced here: 112 us
  Pallas kernels  108 us (95%)
  local copies, waits for them, and re-layouts  2.56 us (2%)
    pallas_call x1, Pallas kernels, on_device(): pl.pallas_call(functools.partial(kernel, n_gx, n_gy, layers, wells), out_...  108 us
    unnamed x4, local copies, waits for them, and re-layouts  2.56 us

profile of v7, /device:TPU:1, one launch (start us, length us, event | category | flops | bytes accessed | tf_op | source)
XLA Modules:
  0.0 111.6 jit_solution(13800573020611855687)
XLA Ops:
  0.6 108.4 %newton.1 = (f32[1024,128]{1,0:T(8,128)}, f32[128,256]{1,0:T(8,128)}) custom-call(f32[1024,128]{1,0:T(8,128)} %bitcast.7, f32[1024,128]{1,0:T(8,128)} %bitcast.8, s32[256,128]{1,0:T(8,128)} %bitcast.10, f32[4,8]{1,0:T(4,128)} %table.1, s32[128,128]{1,0:T(8,128)} %bitcast.11, s32[32,256]{1,0:T(8,128)} %slots_in.1, f32[4,4,32,256]{3,2,1,0:T(8,128)} %inverse_in.1), custom_call_target="tpu_custom_call" | custom-call | tf_op jit(solution)/shard_map/newton/pallas_call | solution.py:539
  109.1 0.0 copy-start
  109.1 1.9 %copy.11 = f32[4,32,8,128]{3,2,1,0:T(8,128)} copy(f32[4,32,8,128]{3,2,1,0:T(8,128)} %bitcast.6) | data formatting | bytes 1048576
  111.0 0.0 copy-done
  111.0 0.7 copy.12
Async XLA Ops:
  109.1 1.9 %copy-start = (f32[128,256]{1,0:T(8,128)S(1)}, f32[128,256]{1,0:T(8,128)}, u32[]{:S(2)}) copy-start(f32[128,256]{1,0:T(8,128)} %get-tuple-element.5) | copy-start | bytes 393220

commit v8 on v7

--- a/solution.py
+++ b/solution.py
@@ -238,7 +238,7 @@
             gather_chunk(chunk)
             return inner
 
-        lax.fori_loop(0, early, early_step, 0)
+        lax.fori_loop(0, early, early_step, 0, unroll=2)
 
         @pl.when(n == 0)
         def _():
@@ -330,7 +330,7 @@
             rows[1, pl.ds(w, 4, stride=wells), :] = value[:, 128:]
             return inner
 
-        lax.fori_loop(0, wells, owner_gather, 0, unroll=8)
+        lax.fori_loop(0, wells, owner_gather, 0, unroll=16)
         flows = []
         for i in range(4):
             sides = []

time: 114 us -> 112 us (0.982)
  Pallas kernels: 108 us -> 106 us
    pallas_call x1, Pallas kernels: 108 us -> 106 us  [on_device(): pl.pallas_call(functools.partial(kernel, n_gx, n_gy, layers, wells), out_...]
where the time goes in v8:
time: 112 us; the launch traced here: 110 us
  Pallas kernels  106 us (95%)
  local copies, waits for them, and re-layouts  2.56 us (2%)
    pallas_call x1, Pallas kernels, on_device(): pl.pallas_call(functools.partial(kernel, n_gx, n_gy, layers, wells), out_...  106 us
    unnamed x4, local copies, waits for them, and re-layouts  2.56 us

profile of v8, /device:TPU:1, one launch (start us, length us, event | category | flops | bytes accessed | tf_op | source)
XLA Modules:
  0.0 109.6 jit_solution(10433998775500564416)
XLA Ops:
  0.6 106.4 %newton.1 = (f32[1024,128]{1,0:T(8,128)}, f32[128,256]{1,0:T(8,128)}) custom-call(f32[1024,128]{1,0:T(8,128)} %bitcast.7, f32[1024,128]{1,0:T(8,128)} %bitcast.8, s32[256,128]{1,0:T(8,128)} %bitcast.10, f32[4,8]{1,0:T(4,128)} %table.1, s32[128,128]{1,0:T(8,128)} %bitcast.11, s32[32,256]{1,0:T(8,128)} %slots_in.1, f32[4,4,32,256]{3,2,1,0:T(8,128)} %inverse_in.1), custom_call_target="tpu_custom_call" | custom-call | tf_op jit(solution)/shard_map/newton/pallas_call | solution.py:539
  107.0 0.0 copy-start
  107.1 1.9 %copy.11 = f32[4,32,8,128]{3,2,1,0:T(8,128)} copy(f32[4,32,8,128]{3,2,1,0:T(8,128)} %bitcast.6) | data formatting | bytes 1048576
  109.0 0.0 copy-done
  109.0 0.7 copy.12
Async XLA Ops:
  107.0 1.9 %copy-start = (f32[128,256]{1,0:T(8,128)S(1)}, f32[128,256]{1,0:T(8,128)}, u32[]{:S(2)}) copy-start(f32[128,256]{1,0:T(8,128)} %get-tuple-element.5) | copy-start | bytes 393220
